TPU v7x, 32 devices: a whole 2x2x4 slice. The times are simulated.
32 devices in a mesh: fsdp: 2 (over x), context: 4 (over y, core), tensor: 4 (over z).
Axes of the slice: x: 2, y: 2, z: 4, core: 2. Of those that a mesh axis runs over, the one named last changes fastest.
Arguments:
- tokens: bfloat16 [2, 2048, 1024], P('fsdp', 'context'), may hold values from -6 to 6
- cotangent: bfloat16 [2, 2048, 1024], P('fsdp', 'context'), may hold values from -6 to 6
- lengths: int32 [2, 4], P('fsdp'), may hold values from 1 to 1024, 2048 in all within a row
- w_in: bfloat16 [3, 1024, 1024], P(None, 'fsdp', 'tensor'), may hold values from -0.1875 to 0.1875
- w_out: bfloat16 [1024, 1024], P('tensor', 'fsdp'), may hold values from -0.1875 to 0.1875
- w_gate_up: bfloat16 [2, 1024, 4608], P(None, 'fsdp', 'tensor'), may hold values from -0.1875 to 0.1875
- w_down: bfloat16 [4608, 1024], P('tensor', 'fsdp'), may hold values from -0.1875 to 0.1875
- norm_gains: bfloat16 [2, 1024], P(None, 'fsdp'), may hold values from 0.5 to 1.5
- conv_kernel: bfloat16 [3, 1024], P(None, 'tensor'), may hold values from -3 to 3
Outputs:
- block_out: float32 [2, 2048, 1024], P('fsdp', 'context')
- grad_tokens: float32 [2, 2048, 1024], P('fsdp', 'context')
- grad_w_in: float32 [3, 1024, 1024], P(None, 'fsdp', 'tensor')
- grad_w_out: float32 [1024, 1024], P('tensor', 'fsdp')
- grad_w_gate_up: float32 [2, 1024, 4608], P(None, 'fsdp', 'tensor')
- grad_w_down: float32 [4608, 1024], P('tensor', 'fsdp')
- grad_norm_gains: float32 [2, 1024], P(None, 'fsdp')
- grad_conv_kernel: float32 [3, 1024], P(None, 'tensor')
Inputs may be any that keep to these rules, and one draw needn't show every extreme that they name: `lengths`: each row of 2048 tokens is a pack of 4 whole documents, in order; some document of every row has 1024 tokens.
All inputs are finite; a program needn't handle non-finite values.
Results may differ from a plain program's by a relative error of at most 0.0088.
Values may be sent and summed in bfloat16 or wider, within the bound.
No kernel may reach another device: no remote copies, remote signals or barrier semaphores. Data moves between devices by JAX's collectives and lax.ppermute only.
A program may use at most 128 MiB of HBM per device.

v0:
```python
import jax
import jax.numpy as jnp
from jax import lax
from jax.sharding import PartitionSpec as P

norm_eps = 1e-05


def shifted(block, axis, distance):
    devices = range(lax.axis_size(axis))
    route = [(i - distance, i) for i in devices if i - distance in devices]
    return lax.ppermute(block, axis, route)


def matmul_plain(matrix_one, matrix_two):
    return jnp.dot(matrix_one, matrix_two, preferred_element_type=jnp.float32)


def matmul_right(matrix_one, matrix_two):
    return lax.dot_general(
        matrix_one, matrix_two, (((1,), (1,)), ((), ())), preferred_element_type=jnp.float32
    )


def matmul_left(matrix_one, matrix_two):
    return lax.dot_general(
        matrix_one, matrix_two, (((0,), (0,)), ((), ())), preferred_element_type=jnp.float32
    )


def norm_forward(values):
    inv_root = lax.rsqrt(jnp.mean(values * values, axis=-1, keepdims=True) + norm_eps)
    return (values * inv_root, inv_root)


def norm_backward(normed, inv_root, gain_row, grad_out):
    grad_normed = grad_out * gain_row
    inner_mean = jnp.mean(grad_normed * normed, axis=-1, keepdims=True)
    return (inv_root * (grad_normed - normed * inner_mean), jnp.sum(grad_out * normed, axis=0))


def keep_masks(position, lengths_row):
    starts = jnp.cumsum(lengths_row) - lengths_row
    doc_start = jnp.max(jnp.where(starts[None, :] <= position[:, None], starts[None, :], 0), axis=1)
    keep_one = (position - 1 >= doc_start).astype(jnp.float32)[:, None]
    keep_two = (position - 2 >= doc_start).astype(jnp.float32)[:, None]
    return (keep_one, keep_two)


def local(tokens, cotangent, lengths, w_in, w_out, w_gate_up, w_down, norm_gains, conv_kernel):
    block_rows = tokens.shape[1]
    position = lax.axis_index("context") * block_rows + jnp.arange(block_rows + 2, dtype=jnp.int32)
    keep_one_ext, keep_two_ext = keep_masks(position, lengths[0])
    keep_one = keep_one_ext[:block_rows]
    keep_two = keep_two_ext[:block_rows]
    full_in, full_out, full_gate_up, full_down, full_gains = (
        lax.all_gather(w_in, "fsdp", axis=1, tiled=True),
        lax.all_gather(w_out, "fsdp", axis=1, tiled=True),
        lax.all_gather(w_gate_up, "fsdp", axis=1, tiled=True),
        lax.all_gather(w_down, "fsdp", axis=1, tiled=True),
        lax.all_gather(norm_gains, "fsdp", axis=1, tiled=True),
    )
    inputs = tokens[0].astype(jnp.float32)
    gain_first = full_gains[0].astype(jnp.float32)
    gain_second = full_gains[1].astype(jnp.float32)
    kernel_taps = conv_kernel.astype(jnp.float32)
    normed_one, root_one = norm_forward(inputs)
    hidden_one = (normed_one * gain_first).astype(jnp.bfloat16)
    b_part = matmul_plain(hidden_one, full_in[0])
    c_part = matmul_plain(hidden_one, full_in[1])
    x_part = matmul_plain(hidden_one, full_in[2])
    mixed = b_part * x_part
    rim_rows = shifted(mixed[-2:], "context", 1)
    extended = jnp.concatenate([rim_rows, mixed], axis=0)
    back_one = extended[1:-1] * keep_one
    back_two = extended[:-2] * keep_two
    conv_value = kernel_taps[2] * mixed + kernel_taps[1] * back_one + kernel_taps[0] * back_two
    gated = (c_part * conv_value).astype(jnp.bfloat16)
    first_sum = inputs + lax.psum(matmul_plain(gated, full_out), "tensor")
    normed_two, root_two = norm_forward(first_sum)
    hidden_two = (normed_two * gain_second).astype(jnp.bfloat16)
    gate_value = matmul_plain(hidden_two, full_gate_up[0])
    up_value = matmul_plain(hidden_two, full_gate_up[1])
    sigmoid_gate = jax.nn.sigmoid(gate_value)
    silu_gate = gate_value * sigmoid_gate
    act_value = (silu_gate * up_value).astype(jnp.bfloat16)
    output_rows = first_sum + lax.psum(matmul_plain(act_value, full_down), "tensor")
    full_in, full_out, full_gate_up, full_down, full_gains = (
        lax.all_gather(w_in, "fsdp", axis=1, tiled=True),
        lax.all_gather(w_out, "fsdp", axis=1, tiled=True),
        lax.all_gather(w_gate_up, "fsdp", axis=1, tiled=True),
        lax.all_gather(w_down, "fsdp", axis=1, tiled=True),
        lax.all_gather(norm_gains, "fsdp", axis=1, tiled=True),
    )
    cot_rows = cotangent[0]
    grad_act = matmul_right(cot_rows, full_down)
    grad_gate = (
        grad_act * up_value * sigmoid_gate * (1.0 + gate_value * (1.0 - sigmoid_gate))
    ).astype(jnp.bfloat16)
    grad_up = (grad_act * silu_gate).astype(jnp.bfloat16)
    grad_h2 = lax.psum(
        matmul_right(grad_gate, full_gate_up[0]) + matmul_right(grad_up, full_gate_up[1]), "tensor"
    )
    back_second, grad_gain_two = norm_backward(normed_two, root_two, gain_second, grad_h2)
    grad_first = cot_rows.astype(jnp.float32) + back_second
    grad_first_b = grad_first.astype(jnp.bfloat16)
    grad_gated = matmul_right(grad_first_b, full_out)
    grad_conv = grad_gated * c_part
    next_rows = shifted(grad_conv[:2], "context", -1)
    ahead = jnp.concatenate([grad_conv, next_rows], axis=0)
    ahead_one = ahead[1 : block_rows + 1] * keep_one_ext[1 : block_rows + 1]
    ahead_two = ahead[2:] * keep_two_ext[2:]
    grad_mixed = (
        kernel_taps[2] * grad_conv + kernel_taps[1] * ahead_one + kernel_taps[0] * ahead_two
    )
    grad_kernel = jnp.stack(
        [
            jnp.sum(grad_conv * back_two, axis=0),
            jnp.sum(grad_conv * back_one, axis=0),
            jnp.sum(grad_conv * mixed, axis=0),
        ]
    )
    grad_b = (grad_mixed * x_part).astype(jnp.bfloat16)
    grad_c = (grad_gated * conv_value).astype(jnp.bfloat16)
    grad_x = (grad_mixed * b_part).astype(jnp.bfloat16)
    local_h1 = (
        matmul_right(grad_b, full_in[0])
        + matmul_right(grad_c, full_in[1])
        + matmul_right(grad_x, full_in[2])
    )
    grad_h1 = lax.psum(local_h1, "tensor")
    back_first, grad_gain_one = norm_backward(normed_one, root_one, gain_first, grad_h1)
    grad_inputs = grad_first + back_first
    term_in = jnp.stack(
        [
            matmul_left(hidden_one, grad_b),
            matmul_left(hidden_one, grad_c),
            matmul_left(hidden_one, grad_x),
        ]
    )
    term_out = matmul_left(gated, grad_first_b)
    term_gate_up = jnp.stack([matmul_left(hidden_two, grad_gate), matmul_left(hidden_two, grad_up)])
    term_down = matmul_left(act_value, cot_rows)
    term_gains = jnp.stack([grad_gain_one, grad_gain_two])
    pieces = (
        lax.psum_scatter(term_in, "fsdp", scatter_dimension=1, tiled=True),
        lax.psum_scatter(term_out, "fsdp", scatter_dimension=1, tiled=True),
        lax.psum_scatter(term_gate_up, "fsdp", scatter_dimension=1, tiled=True),
        lax.psum_scatter(term_down, "fsdp", scatter_dimension=1, tiled=True),
        lax.psum_scatter(term_gains, "fsdp", scatter_dimension=1, tiled=True),
    )
    reduced = lax.psum((pieces[0], pieces[1], pieces[2], pieces[3], pieces[4]), "context")
    kernel_total = lax.psum(grad_kernel, ("fsdp", "context"))
    return (
        output_rows[None],
        grad_inputs[None],
        reduced[0],
        reduced[1],
        reduced[2],
        reduced[3],
        reduced[4],
        kernel_total,
    )


def solution(mesh):
    placed = (
        P("fsdp", "context", None),
        P("fsdp", "context", None),
        P("fsdp", None),
        P(None, "fsdp", "tensor"),
        P("tensor", "fsdp"),
        P(None, "fsdp", "tensor"),
        P("tensor", "fsdp"),
        P(None, "fsdp"),
        P(None, "tensor"),
    )
    return jax.shard_map(
        local,
        mesh=mesh,
        in_specs=placed,
        out_specs=(
            P("fsdp", "context", None),
            P("fsdp", "context", None),
            P(None, "fsdp", "tensor"),
            P("tensor", "fsdp"),
            P(None, "fsdp", "tensor"),
            P("tensor", "fsdp"),
            P(None, "fsdp"),
            P(None, "tensor"),
        ),
        check_vma=False,
    )
```

profile of v0, /device:TPU:0, one launch (start us, length us, event | category | flops | bytes accessed | tf_op | source)
XLA Modules:
  0.0 958.6 jit_solution(321070914398784171)
XLA Ops:
  9.4 5.5 all_gather.19
  15.0 1.6 fusion.15
  17.5 21.9 %all-gather.4.cloned.1.call-done = bf16[3,1024,256]{2,1,0:T(8,128)(2,1)} async-done(((bf16[3,512,256]{2,1,0:T(8,128)(2,1)}), bf16[3,1024,256]{2,1,0:T(8,128)(2,1)}) %all-gather.4.cloned.1.call-update) | async-done | bytes 1572880 | tf_op jit(solution)/shard_map/all_gather | solution.py:57
  39.5 2.0 fusion.46
  41.5 1.3 fusion.60
  42.8 1.6 collective-permute-start
  44.4 8.9 all_gather.21
  53.3 1.6 multiply_convert_fusion.7
  55.6 1.8 fusion.61
  58.7 84.5 %all-reduce.7.cloned.1.call-done = f32[512,1024]{1,0:T(8,128)} async-done(((f32[512,1024]{1,0:T(8,128)}), f32[512,1024]{1,0:T(8,128)}) %all-reduce.7.cloned.1.call-update) | async-done | bytes 2097168 | tf_op jit(solution)/shard_map/psum | solution.py:79
  143.2 1.9 multiply_reduce_fusion.2
  145.1 1.3 multiply_convert_fusion.3
  146.4 60.0 %all-gather.6.cloned.1.call-done = bf16[2,1024,1152]{2,1,0:T(8,128)(2,1)} async-done(((bf16[2,512,1152]{2,1,0:T(8,128)(2,1)}), bf16[2,1024,1152]{2,1,0:T(8,128)(2,1)}) %all-gather.6.cloned.1.call-update) | async-done | bytes 4718608 | tf_op jit(solution)/shard_map/all_gather | solution.py:59
  206.4 5.1 fusion.19
  211.5 2.9 fusion.21
  214.4 29.5 %all-gather.8.cloned.1.call-done = bf16[1152,1024]{1,0:T(8,128)(2,1)} async-done(((bf16[1152,512]{1,0:T(8,128)(2,1)}), bf16[1152,1024]{1,0:T(8,128)(2,1)}) %all-gather.8.cloned.1.call-update) | async-done | bytes 2359312 | tf_op jit(solution)/shard_map/all_gather | solution.py:60
  243.9 6.7 multiply_convert_fusion
  250.6 4.1 fusion.18
  254.6 4.5 fusion.22
  259.4 4.9 fusion.62
  264.3 81.2 %all-reduce.9.cloned.1.call-done = f32[512,1024]{1,0:T(8,128)} async-done(((f32[512,1024]{1,0:T(8,128)}), f32[512,1024]{1,0:T(8,128)}) %all-reduce.9.cloned.1.call-update) | async-done | bytes 2097168 | tf_op jit(solution)/shard_map/psum | solution.py:101
  345.5 2.3 multiply_reduce_fusion
  351.5 1.4 collective-permute-start.1
  353.4 1.3 collective-permute-done.1
  356.3 1.8 add_add_fusion
  358.2 3.2 fusion.38
  361.4 1.6 convolution_bitcast_fusion.3
  364.7 1.8 pad_maximum_fusion.1
  366.6 5.2 fusion.24
  371.8 3.3 convolution_bitcast_fusion
  375.2 1.6 convolution_bitcast_fusion.1
  376.7 4.3 pad_maximum_fusion
  381.3 131.5 %all-reduce.11.cloned.1.call-done = (f32[512,1024]{1,0:T(8,128)}, f32[512,1024]{1,0:T(8,128)}) async-done(((f32[512,1024]{1,0:T(8,128)}, f32[512,1024]{1,0:T(8,128)}), (f32[512,1024]{1,0:T(8,128)}, f32[512,1024]{1,0:T(8,128)})) %all-reduce.11.cloned.1.call-update) | async-done | bytes 4194320 | tf_op jit(solution)/shard_map/psum | solution.py:87
  512.8 2.2 fusion.14
  515.1 1.0 copy.17
  516.2 18.3 %reduce-scatter.10.cloned.1.call-done = f32[256,512]{1,0:T(8,128)} async-done(((f32[256,1024]{1,0:T(8,128)}), f32[256,512]{1,0:T(8,128)}) %reduce-scatter.10.cloned.1.call-update) | async-done | bytes 524304 | tf_op jit(solution)/shard_map/reduce_scatter | solution.py:147
  534.4 45.7 %reduce-scatter.8.cloned.1.call-done = f32[3,512,256]{2,1,0:T(8,128)} async-done(((f32[3,1024,256]{2,1,0:T(8,128)}), f32[3,512,256]{2,1,0:T(8,128)}) %reduce-scatter.8.cloned.1.call-update) | async-done | bytes 1572880 | tf_op jit(solution)/shard_map/reduce_scatter | solution.py:146
  580.1 63.0 %reduce-scatter.14.cloned.1.call-done = f32[1152,512]{1,0:T(8,128)} async-done(((f32[1152,1024]{1,0:T(8,128)}), f32[1152,512]{1,0:T(8,128)}) %reduce-scatter.14.cloned.1.call-update) | async-done | bytes 2359312 | tf_op jit(solution)/shard_map/reduce_scatter | solution.py:149
  643.1 112.8 %reduce-scatter.12.cloned.1.call-done = f32[2,512,1152]{2,1,0:T(8,128)} async-done(((f32[2,1024,1152]{2,1,0:T(8,128)}), f32[2,512,1152]{2,1,0:T(8,128)}) %reduce-scatter.12.cloned.1.call-update) | async-done | bytes 4718608 | tf_op jit(solution)/shard_map/reduce_scatter | solution.py:148
  756.0 13.1 %psum.79 = f32[3,256]{1,0:T(4,128)} all-reduce(f32[3,256]{1,0:T(4,128)S(1)} %pad_maximum_fusion.5), channel_id=1, replica_groups=mesh['fsdp'=2,'context'=4,'tensor'=4] {'fsdp','context'}, use_global_device_ids=true, to_apply=%region_25.26 | all-reduce | flops 768 | bytes 6144 | tf_op jit(solution)/shard_map/psum | solution.py:153
  769.1 3.6 add_bitcast_fusion
  772.8 1.9 fusion.12
  774.7 1.1 copy.18
  775.8 6.3 psum.78
  782.1 159.7 %all-reduce.13.cloned.1.call-done = (f32[3,512,256]{2,1,0:T(8,128)}, f32[256,512]{1,0:T(8,128)}, f32[2,512,1152]{2,1,0:T(8,128)}, f32[1152,512]{1,0:T(8,128)}) async-done(((f32[3,512,256]{2,1,0:T(8,128)}, f32[256,512]{1,0:T(8,128)}, f32[2,512,1152]{2,1,0:T(8,128)}, f32[1152,512]{1,0:T(8,128)}), (f32[3,512,256]{2,1,0:T(8,128)}, f32[256,512]{1,0:T(8,128)}, f32[2,512,1152]{2,1,0:T(8,128)}, ...) | async-done | bytes 9175056 | tf_op jit(solution)/shard_map/psum | solution.py:152
  941.8 2.7 copy.27
  945.3 5.0 copy.29
  950.3 1.4 copy.30
  (112 shorter events, 14.2 us)
Async XLA Ops:
  7.2 32.3 %all-gather.4.cloned.1.call-start = ((), (), s32[]{:S(2)}) async-start(), calls=%async_computation.5 | async-start | bytes 2359296 | tf_op jit(solution)/shard_map/all_gather | solution.py:57
  7.9 135.3 %all-reduce.7.cloned.1.call-start = ((), (), s32[]{:S(2)}) async-start(), calls=%async_computation.6 | async-start | bytes 4194304 | tf_op jit(solution)/shard_map/psum | solution.py:79
  15.0 26.4 %copy-start.2 = (bf16[1,512,1024]{2,1,0:T(8,128)(2,1)S(1)}, bf16[1,512,1024]{2,1,0:T(8,128)(2,1)}, u32[]{:S(2)}) copy-start(bf16[1,512,1024]{2,1,0:T(8,128)(2,1)} %param.9) | copy-start | bytes 3145732
  39.5 2.0 copy-start.11
  41.5 1.3 copy-start.23
  41.5 2.9 copy-start.28
  42.8 12.1 %copy-start.20 = (f32[512,256]{1,0:T(8,128)}, f32[512,256]{1,0:T(8,128)S(1)}, u32[]{:S(2)}) copy-start(f32[512,256]{1,0:T(8,128)S(1)} %get-tuple-element.43) | copy-start | bytes 1572868
  42.8 10.5 %collective-permute-start = (f32[2,256]{1,0:T(2,128)S(1)}, f32[2,256]{1,0:T(2,128)S(1)}, u32[]{:S(2)}, u32[]{:S(2)}) collective-permute-start(f32[2,256]{1,0:T(2,128)S(1)} %slice.98), channel_id=1, source_target_pairs={{0,4},{4,8},{8,12},{1,5},{5,9},{9,13},{2,6},{6,10},{10,14},{3,7},{... | collective-permute-start | bytes 6152 | tf_op jit(solution)/shard_map/ppermute | solution.py:12
  53.3 1.6 copy-start.7
  54.9 0.7 copy-start.18
  57.3 149.1 %all-gather.6.cloned.1.call-start = ((), (), s32[]{:S(2)}) async-start(), calls=%async_computation.7 | async-start | bytes 7077888 | tf_op jit(solution)/shard_map/all_gather | solution.py:59
  58.1 185.8 %all-gather.8.cloned.1.call-start = ((), (), s32[]{:S(2)}) async-start(), calls=%async_computation.8 | async-start | bytes 3538944 | tf_op jit(solution)/shard_map/all_gather | solution.py:60
  58.7 286.9 %all-reduce.9.cloned.1.call-start = ((), (), s32[]{:S(2)}) async-start(), calls=%async_computation.9 | async-start | bytes 4194304 | tf_op jit(solution)/shard_map/psum | solution.py:101
  206.4 5.1 copy-start.3
  206.4 5.1 copy-start.29
  250.5 4.1 copy-start.13
  250.5 4.1 copy-start.15
  259.2 253.6 %all-reduce.11.cloned.1.call-start = ((), (), s32[]{:S(2)}) async-start(), calls=%async_computation.15 | async-start | bytes 8388608 | tf_op jit(solution)/shard_map/psum | solution.py:87
  345.5 2.3 copy-start.5
  345.5 2.5 copy-start.9
  348.0 1.0 copy-start.8
  349.1 2.4 copy-start
  349.1 1.4 copy-start.21
  349.1 2.0 copy-start.26
  349.1 2.1 copy-start.27
  349.6 3.4 copy-start.12
  351.5 3.5 copy-start.19
  351.5 3.2 copy-start.22
  351.5 3.2 collective-permute-start.1
  353.0 2.0 copy-start.24
  355.1 0.7 copy-start.16
  358.1 176.3 %reduce-scatter.10.cloned.1.call-start = ((), (), s32[]{:S(2)}) async-start(), calls=%async_computation.11 | async-start | bytes 1572864 | tf_op jit(solution)/shard_map/reduce_scatter | solution.py:147
  361.4 218.7 %reduce-scatter.8.cloned.1.call-start = ((), (), s32[]{:S(2)}) async-start(), calls=%async_computation.10 | async-start | bytes 4718592 | tf_op jit(solution)/shard_map/reduce_scatter | solution.py:146
  363.0 1.0 copy-start.17
  366.5 276.6 %reduce-scatter.14.cloned.1.call-start = ((), (), s32[]{:S(2)}) async-start(), calls=%async_computation.13 | async-start | bytes 7077888 | tf_op jit(solution)/shard_map/reduce_scatter | solution.py:149
  371.8 384.2 %reduce-scatter.12.cloned.1.call-start = ((), (), s32[]{:S(2)}) async-start(), calls=%async_computation.12 | async-start | bytes 14155776 | tf_op jit(solution)/shard_map/reduce_scatter | solution.py:148
  371.8 3.3 copy-start.4
  371.8 3.3 copy-start.14
  381.0 393.7 %reduce-scatter.16.cloned.1.call-start = ((), (), s32[]{:S(2)}) async-start(), calls=%async_computation.14 | async-start | bytes 786432
  516.1 425.7 %all-reduce.13.cloned.1.call-start = ((), (), s32[]{:S(2)}) async-start(), calls=%async_computation.16 | async-start | bytes 18350080 | tf_op jit(solution)/shard_map/psum | solution.py:152
  769.1 3.6 copy-start.1
  769.1 3.6 copy-start.6
  941.8 2.7 copy-start.25
  945.3 5.0 copy-start.10
Sparse Core Ops, SparseCore 0:
  9.5 29.8 all-gather.3
  57.5 85.6 all-reduce.6
  144.7 61.6 all-gather.5
  207.8 36.0 all-gather.7
  259.3 86.1 all-reduce.8
  358.2 154.5 all-reduce.10
  515.0 19.3 reduce-scatter.9
  536.7 43.3 reduce-scatter.7
  583.0 60.0 reduce-scatter.13
  645.3 110.6 reduce-scatter.11
  758.8 14.6 reduce-scatter.15
  776.1 165.6 all-reduce.12
where the time goes:
time: 959 us
  waiting for transfers between devices  811 us (85%)
  matrix products  54 us (6%)
  blocking collectives  33.8 us (4%)
  other arithmetic  23.9 us (2%)
  local copies, waits for them, and re-layouts  17 us (2%)
  between operations  14.6 us (2%)
    psum x1, waiting for transfers between devices, local(): lax.psum((pieces[0], pieces[1], pieces[2], pieces[3], pieces[4]), 'context')  160 us
    psum x1, waiting for transfers between devices, local(): lax.psum(matmul_plain(act_value, full_down), 'tensor')  131 us
    reduce_scatter x1, waiting for transfers between devices, local(): lax.psum_scatter(term_gate_up, 'fsdp', scatter_dimension=1, tiled=True)  113 us
    psum x1, waiting for transfers between devices, local(): first_sum = inputs + lax.psum(matmul_plain(gated, full_out), 'tensor')  84.5 us
    psum x1, waiting for transfers between devices, local(): lax.psum(matmul_right(grad_gate, full_gate_up[0]) + matmul_right(grad_up,...  81.2 us
    reduce_scatter x1, waiting for transfers between devices, local(): lax.psum_scatter(term_down, 'fsdp', scatter_dimension=1, tiled=True)  63 us
    all_gather x1, waiting for transfers between devices, local(): lax.all_gather(w_gate_up, 'fsdp', axis=1, tiled=True)  60 us
    reduce_scatter x1, waiting for transfers between devices, local(): lax.psum_scatter(term_in, 'fsdp', scatter_dimension=1, tiled=True)  45.7 us
  transfers between devices with their start and end apart: 14, of which 12 were waited for; matrix products, arithmetic and copies ran while one was open for 5% of the time, Pallas kernels for 0%

commit v1 on v0

v1 whole, which is shorter than its diff:
```python
import jax
import jax.numpy as jnp
from jax import lax
from jax.experimental import pallas as pl
from jax.experimental.pallas import tpu as pltpu
from jax.sharding import PartitionSpec as P


norm_eps = 1e-05
f32 = jnp.float32
bf16 = jnp.bfloat16
halo = 16


def swap(block, axis, mask):
    return lax.ppermute(block, axis, [(i, i ^ mask) for i in range(lax.axis_size(axis))])


def after(value, *deps):
    return lax.optimization_barrier((value,) + deps)[0]


def shifted(block, axis, distance):
    devices = range(lax.axis_size(axis))
    return lax.ppermute(block, axis, [(i - distance, i) for i in devices if i - distance in devices])


def dot(a, b):
    return jnp.dot(a, b, preferred_element_type=f32)


def dot_right(a, b):
    return lax.dot_general(a, b, (((1,), (1,)), ((), ())), preferred_element_type=f32)


def dot_left(a, b):
    return lax.dot_general(a, b, (((0,), (0,)), ((), ())), preferred_element_type=f32)


def fetch_shards(shard, cut):
    core = lax.axis_index("context") % 2
    half = shard.shape[cut] // 2
    mine = lax.dynamic_slice_in_dim(shard, core * half, half, cut)
    return [swap(mine, "fsdp", mask) for mask in range(1, lax.axis_size("fsdp"))]


def swap_cores(pieces):
    return [swap(piece, "context", 1) for piece in pieces]


def tensor_swap(blocks):
    return [swap(blocks[mask], "tensor", mask) for mask in range(1, len(blocks))]


def call(body, outs, ins, scratch=(), any_ins=(), flops=0):
    size = lambda a: a.size * a.dtype.itemsize
    kernel = pl.pallas_call(
        body,
        out_shape=[jax.ShapeDtypeStruct(s, d) for s, d in outs],
        in_specs=[
            pl.BlockSpec(memory_space=pltpu.SMEM if a.dtype == jnp.int32 else pltpu.VMEM)
            for a in ins
        ]
        + [pl.BlockSpec(memory_space=pl.ANY) for _ in any_ins],
        out_specs=[pl.BlockSpec(memory_space=pltpu.VMEM) for _ in outs],
        scratch_shapes=list(scratch),
        compiler_params=pltpu.CompilerParams(vmem_limit_bytes=56 << 20),
        cost_estimate=pl.CostEstimate(
            flops=flops,
            transcendentals=0,
            bytes_accessed=sum(size(a) for a in list(ins) + list(any_ins)),
        ),
    )
    return kernel(*ins, *any_ins)


def mult(value, by):
    return pl.multiple_of(value, by)


def shard_places(shape, dim, cut, n_fs):
    me, core = lax.axis_index("fsdp"), lax.axis_index("context") % 2
    size, half = shape[dim], shape[cut] // 2

    def place(owner, part):
        index = []
        for axis, extent in enumerate(shape):
            start, length, unit = 0, extent, extent
            if axis == dim:
                start, unit = owner * size, size
            if axis == cut and part is not None:
                start, length, unit = start + part * half, half, half
            index.append(slice(None) if isinstance(start, int) else pl.ds(mult(start, unit), length))
        return tuple(index)

    own = [place(me, None)]
    firsts = [place(me ^ mask, core) for mask in range(1, n_fs)]
    seconds = [place(me ^ mask, 1 - core) for mask in range(1, n_fs)]
    return own + firsts + seconds


class Assembled:
    def __init__(self, pieces, dim, cut, n_fs):
        self.pieces, self.dim, self.cut, self.n_fs = pieces, dim, cut, n_fs
        self.local = pieces[0].shape
        self.shape = tuple(
            s * n_fs if axis == dim else s for axis, s in enumerate(self.local)
        )
        self.count = len(pieces)

    def scratch(self):
        return [pltpu.VMEM(self.shape, bf16), pltpu.SemaphoreType.DMA((self.count,))]

    def copies(self, refs, whole, sems):
        places = shard_places(self.local, self.dim, self.cut, self.n_fs)
        return [
            pltpu.make_async_copy(ref, whole.at[place], sems.at[i])
            for i, (ref, place) in enumerate(zip(refs, places))
        ]


def row_rms(v):
    return lax.rsqrt(jnp.mean(v * v, axis=-1, keepdims=True) + norm_eps)


def keeps(lengths_ref, first, shape):
    position = first + lax.broadcasted_iota(jnp.int32, shape, 0)
    start = jnp.int32(0)
    one = jnp.ones(shape, jnp.bool_)
    two = jnp.ones(shape, jnp.bool_)
    for doc in range(lengths_ref.shape[1]):
        one = one & (position != start)
        two = two & (position != start + 1)
        start = start + lengths_ref[0, doc]
    two = two & one
    return one.astype(f32), two.astype(f32)


def split_rows(ref, outs, z):
    rows = outs[0].shape[0]
    for mask, out in enumerate(outs):
        out[...] = ref[pl.ds(mult((z ^ mask) * rows, rows), rows), :]


def join_rows(ref, blocks, z):
    rows = blocks[0].shape[0]
    for mask, block in enumerate(blocks):
        ref[pl.ds(mult((z ^ mask) * rows, rows), rows), :] = block[...].astype(ref.dtype)


def mixer_forward(lengths, tokens, before, behind, gains, taps, w_in, w_out, nz):
    rows, width = tokens.shape
    chan = w_in.local[2]
    ext = rows + 2 * halo
    share = rows // nz

    def body(*refs):
        len_ref, tok, prev, nxt, gain, tap = refs[:6]
        refs = refs[6:]
        in_refs, refs = refs[: w_in.count], refs[w_in.count :]
        out_refs, refs = refs[: w_out.count], refs[w_out.count :]
        parts, refs = refs[:nz], refs[nz:]
        h_out, b_out, c_out, x_out, gated_out = refs[:5]
        win, sem_in, wout, sem_out, hid, mixed, whole = refs[5:]
        z, ctx = lax.axis_index("tensor"), lax.axis_index("context")
        copy_in = w_in.copies(in_refs, win, sem_in)
        copy_out = w_out.copies(out_refs, wout, sem_out)
        for copy in copy_in + copy_out:
            copy.start()
        g = gain[...].astype(f32)

        def hidden(v):
            v = v.astype(f32)
            return (v * row_rms(v) * g).astype(bf16)

        hid[:halo, :] = hidden(prev[...])
        hid[halo + rows :, :] = hidden(nxt[...])
        body_rows = hidden(tok[...])
        hid[halo : halo + rows, :] = body_rows
        h_out[...] = body_rows
        for copy in copy_in:
            copy.wait()
        h = hid[...]
        b = dot(h, win[0])
        x = dot(h, win[2])
        c = dot(h, win[1])
        b_out[...] = b
        x_out[...] = x
        c_out[...] = c
        mixed[...] = b * x
        one, two = keeps(len_ref, ctx * rows, (rows, chan))
        t = tap[...].astype(f32)
        conv = (
            t[2:3] * mixed[halo : halo + rows, :]
            + t[1:2] * (mixed[halo - 1 : halo + rows - 1, :] * one)
            + t[0:1] * (mixed[halo - 2 : halo + rows - 2, :] * two)
        )
        gated = (c[halo : halo + rows] * conv).astype(bf16)
        gated_out[...] = gated
        for copy in copy_out:
            copy.wait()
        whole[...] = dot(gated, wout[...]).astype(bf16)
        split_rows(whole, parts, z)

    return call(
        body,
        [((share, width), bf16)] * nz
        + [((rows, width), bf16)]
        + [((ext, chan), f32)] * 3
        + [((rows, chan), bf16)],
        [lengths, tokens, before, behind, gains, taps],
        w_in.scratch()
        + w_out.scratch()
        + [
            pltpu.VMEM((ext, width), bf16),
            pltpu.VMEM((ext, chan), f32),
            pltpu.VMEM((rows, width), bf16),
        ],
        w_in.pieces + w_out.pieces,
        flops=8 * rows * width * chan,
    )


def first_norm(own, received, tokens, gains):
    share, width = own.shape

    def body(*refs):
        own_ref = refs[0]
        others, refs = refs[1 : 1 + len(received)], refs[1 + len(received) :]
        tok, gain, x1_out, h2_out = refs
        z = lax.axis_index("tensor")
        total = tok[pl.ds(mult(z * share, share), share), :].astype(f32)
        total = total + own_ref[...].astype(f32)
        for other in others:
            total = total + other[...].astype(f32)
        x1_out[...] = total
        h2_out[...] = (total * row_rms(total) * gain[...].astype(f32)).astype(bf16)

    return call(
        body, [((share, width), f32), ((share, width), bf16)], [own, *received, tokens, gains]
    )


def feed_forward(own, received, cot, w_gate_up, w_down, nz):
    rows, width = cot.shape
    share = rows // nz
    hidden = w_gate_up.shape[2]
    tile = next(t for t in (384, 256, 128, hidden) if hidden % t == 0)

    def body(*refs):
        blocks, refs = refs[:nz], refs[nz:]
        cot_ref, refs = refs[0], refs[1:]
        gu_refs, refs = refs[: w_gate_up.count], refs[w_gate_up.count :]
        d_refs, refs = refs[: w_down.count], refs[w_down.count :]
        parts, refs = refs[:nz], refs[nz:]
        h2_out, gg_out, gu_out, act_out = refs[:4]
        wgu, sem_gu, wd, sem_d, acc = refs[4:]
        z = lax.axis_index("tensor")
        copy_d = w_down.copies(d_refs, wd, sem_d)
        copy_gu = w_gate_up.copies(gu_refs, wgu, sem_gu)
        for copy in copy_d + copy_gu:
            copy.start()
        join_rows(h2_out, blocks, z)
        acc[...] = jnp.zeros_like(acc)
        for copy in copy_d + copy_gu:
            copy.wait()

        @pl.loop(0, hidden // tile)
        def _(step):
            columns = pl.ds(mult(step * tile, tile), tile)
            h2 = h2_out[...]
            wg, wu = wgu[0, :, columns], wgu[1, :, columns]
            grad_act = dot_right(cot_ref[...], wd[columns, :])
            gate = dot(h2, wg)
            up = dot(h2, wu)
            sig = jax.nn.sigmoid(gate)
            silu = gate * sig
            act_out[:, columns] = (silu * up).astype(bf16)
            gg = (grad_act * up * sig * (1.0 + gate * (1.0 - sig))).astype(bf16)
            gu = (grad_act * silu).astype(bf16)
            gg_out[:, columns] = gg
            gu_out[:, columns] = gu
            acc[...] += dot_right(gg, wg) + dot_right(gu, wu)

        for mask, part in enumerate(parts):
            part[...] = acc[pl.ds(mult((z ^ mask) * share, share), share), :].astype(bf16)

    return call(
        body,
        [((share, width), bf16)] * nz + [((rows, width), bf16)] + [((rows, hidden), bf16)] * 3,
        [own, *received, cot],
        w_gate_up.scratch() + w_down.scratch() + [pltpu.VMEM((rows, width), f32)],
        w_gate_up.pieces + w_down.pieces,
        flops=10 * rows * width * hidden,
    )


def down_product(act, w_down, nz):
    rows, hidden = act.shape
    width = w_down.shape[1]
    share = rows // nz

    def body(*refs):
        act_ref, refs = refs[0], refs[1:]
        d_refs, refs = refs[: w_down.count], refs[w_down.count :]
        parts, (wd, sem_d, whole) = refs[:nz], refs[nz:]
        z = lax.axis_index("tensor")
        copies = w_down.copies(d_refs, wd, sem_d)
        for copy in copies:
            copy.start()
        for copy in copies:
            copy.wait()
        whole[...] = dot(act_ref[...], wd[...]).astype(bf16)
        split_rows(whole, parts, z)

    return call(
        body,
        [((share, width), bf16)] * nz,
        [act],
        w_down.scratch() + [pltpu.VMEM((rows, width), bf16)],
        w_down.pieces,
        flops=2 * rows * width * hidden,
    )


def norm_back(own, received, values, gains, base):
    share, width = own.shape
    n = len(received)
    whole_values, whole_base = values.shape[0] != share, base.shape[0] != share

    def body(*refs):
        own_ref, others, refs = refs[0], refs[1 : 1 + n], refs[1 + n :]
        val, gain, add, out, out_b, grad_gain = refs
        z = lax.axis_index("tensor")
        mine = pl.ds(mult(z * share, share), share)
        e = own_ref[...].astype(f32)
        for other in others:
            e = e + other[...].astype(f32)
        v = (val[mine, :] if whole_values else val[...]).astype(f32)
        start = (add[mine, :] if whole_base else add[...]).astype(f32)
        r = row_rms(v)
        normed = v * r
        eg = e * gain[...].astype(f32)
        inner = jnp.mean(eg * normed, axis=-1, keepdims=True)
        total = start + r * (eg - normed * inner)
        out[...] = total
        out_b[...] = total.astype(bf16)
        grad_gain[...] = jnp.sum(e * normed, axis=0, keepdims=True)

    return call(
        body,
        [((share, width), f32), ((share, width), bf16), ((1, width), f32)],
        [own, *received, values, gains, base],
    )


def mixer_backward(lengths, own, received, halos, b_ext, c_ext, x_ext, taps, w_in, w_out, nz):
    share, width = own.shape
    rows = share * nz
    chan = w_in.local[2]
    ext = rows + halo

    def body(*refs):
        len_ref, refs = refs[0], refs[1:]
        blocks, refs = refs[:nz], refs[nz:]
        ahead, refs = refs[:nz], refs[nz:]
        b_ref, c_ref, x_ref, tap = refs[:4]
        refs = refs[4:]
        in_refs, refs = refs[: w_in.count], refs[w_in.count :]
        out_refs, refs = refs[: w_out.count], refs[w_out.count :]
        parts, refs = refs[:nz], refs[nz:]
        gx_out, gb_out, gc_out, gxx_out, tap_out = refs[:5]
        win, sem_in, wout, sem_out, gx, keep1, keep2, mixed = refs[5:]
        z, ctx = lax.axis_index("tensor"), lax.axis_index("context")
        copy_out = w_out.copies(out_refs, wout, sem_out)
        copy_in = w_in.copies(in_refs, win, sem_in)
        for copy in copy_out + copy_in:
            copy.start()
        join_rows(gx, blocks, z)
        gx_out[...] = gx[:rows, :]
        tail = ahead[0][...]
        for mask in range(1, nz):
            tail = jnp.where(z == mask, ahead[mask][...], tail)
        gx[rows:, :] = tail
        one, two = keeps(len_ref, ctx * rows, (ext, chan))
        t = tap[...].astype(f32)
        mixed[...] = b_ref[: halo + rows, :] * x_ref[: halo + rows, :]
        here = mixed[halo:, :]
        back1 = mixed[halo - 1 : halo + rows - 1, :] * one[:rows]
        back2 = mixed[halo - 2 : halo + rows - 2, :] * two[:rows]
        conv = t[2:3] * here + t[1:2] * back1 + t[0:1] * back2
        for copy in copy_out:
            copy.wait()
        grad_gated = dot_right(gx[...], wout[...])
        grad_conv_ext = grad_gated * c_ref[halo:, :]
        grad_conv = grad_conv_ext[:rows]
        keep1[...] = grad_conv_ext * one
        keep2[...] = grad_conv_ext * two
        grad_mixed = (
            t[2:3] * grad_conv + t[1:2] * keep1[1 : rows + 1, :] + t[0:1] * keep2[2 : rows + 2, :]
        )
        gb = (grad_mixed * x_ref[halo : halo + rows, :]).astype(bf16)
        gc = (grad_gated[:rows] * conv).astype(bf16)
        gxx = (grad_mixed * b_ref[halo : halo + rows, :]).astype(bf16)
        gb_out[...] = gb
        gc_out[...] = gc
        gxx_out[...] = gxx
        tap_out[0:1, :] = jnp.sum(grad_conv * back2, axis=0, keepdims=True)
        tap_out[1:2, :] = jnp.sum(grad_conv * back1, axis=0, keepdims=True)
        tap_out[2:3, :] = jnp.sum(grad_conv * here, axis=0, keepdims=True)
        for copy in copy_in:
            copy.wait()
        total = dot_right(gb, win[0]) + dot_right(gc, win[1]) + dot_right(gxx, win[2])
        gx[:rows, :] = total.astype(bf16)
        split_rows(gx, parts, z)

    return call(
        body,
        [((share, width), bf16)] * nz
        + [((rows, width), bf16)]
        + [((rows, chan), bf16)] * 3
        + [((3, chan), f32)],
        [lengths, own, *received, *halos, b_ext, c_ext, x_ext, taps],
        w_in.scratch()
        + w_out.scratch()
        + [
            pltpu.VMEM((ext, width), bf16),
            pltpu.VMEM((ext, chan), f32),
            pltpu.VMEM((ext, chan), f32),
            pltpu.VMEM((ext, chan), f32),
        ],
        w_in.pieces + w_out.pieces,
        flops=8 * rows * width * chan,
    )


def add_rows(values, own, received):
    def body(*refs):
        total = refs[0][...]
        for ref in refs[1:-1]:
            total = total + ref[...].astype(f32)
        refs[-1][...] = total.astype(bf16)

    return call(body, [(own.shape, bf16)], [values, own, *received])[0]


def widen(own, received, nz):
    share, width = own.shape

    def body(*refs):
        join_rows(refs[-1], refs[:-1], lax.axis_index("tensor"))

    return call(body, [((share * nz, width), f32)], [own, *received])[0]


def part(value, axis, count, index):
    size = value.shape[axis] // count
    return lax.dynamic_slice_in_dim(value, index * size, size, axis)


def fold(value, axis, count, index, name, scale):
    total = part(value, axis, count, index).astype(f32)
    for mask in range(1, count):
        piece = part(value, axis, count, index ^ mask).astype(bf16)
        total = total + swap(piece, name, mask * scale).astype(f32)
    return total


def spread(piece, axis, count, index, name, scale):
    shape = list(piece.shape)
    shape[axis] *= count
    full = jnp.zeros(shape, piece.dtype)
    size = piece.shape[axis]
    full = lax.dynamic_update_slice_in_dim(full, piece, index * size, axis)
    for mask in range(1, count):
        full = lax.dynamic_update_slice_in_dim(
            full, swap(piece, name, mask * scale), (index ^ mask) * size, axis
        )
    return full


class Reduction:
    def __init__(self, partial, dim, cut):
        self.fs, ctx = lax.axis_index("fsdp"), lax.axis_index("context")
        self.n_fs, self.n_rest = lax.axis_size("fsdp"), lax.axis_size("context") // 2
        self.core, self.rest = ctx % 2, ctx // 2
        self.dim, self.cut, self.value = dim, cut, partial

    def over_cores(self):
        dim = self.dim
        if dim == self.cut:
            shape = self.value.shape
            self.size = shape[dim] // self.n_fs
            wide = self.value.reshape(shape[:dim] + (self.n_fs, self.size) + shape[dim + 1 :])
            self.value = fold(wide, dim + 1, 2, self.core, "context", 1)
        else:
            self.value = fold(self.value, self.cut, 2, self.core, "context", 1)

    def over_fsdp(self):
        dim = self.dim
        self.value = fold(self.value, dim, self.n_fs, self.fs, "fsdp", 1)
        if dim == self.cut:
            shape = self.value.shape
            self.value = self.value.reshape(shape[:dim] + (shape[dim + 1],) + shape[dim + 2 :])

    def over_rest(self):
        value = fold(self.value, self.cut, self.n_rest, self.rest, "context", 2)
        self.value = value.astype(bf16)

    def spread_rest(self):
        self.value = spread(self.value, self.cut, self.n_rest, self.rest, "context", 2)

    def spread_cores(self):
        return join_cores(self.value, swap(self.value, "context", 1), self.cut)


def join_cores(own, other, cut):
    half = own.shape[cut]
    shape = tuple(2 * s if axis == cut else s for axis, s in enumerate(own.shape))

    def body(own_ref, other_ref, out_ref):
        core = lax.axis_index("context") % 2
        for ref, owner in ((own_ref, core), (other_ref, 1 - core)):
            index = [slice(None)] * len(shape)
            index[cut] = pl.ds(mult(owner * half, half), half)
            out_ref[tuple(index)] = ref[...].astype(f32)

    return call(body, [(shape, f32)], [own, other])[0]


def sum_blocks(own, received):
    terms = [own, *received]
    while len(terms) > 1:
        terms = [terms[i] + terms[i + 1] for i in range(0, len(terms), 2)]
    return terms[0]


def butterfly(value, axis):
    mask = 1
    while mask < lax.axis_size(axis):
        value = value + swap(value, axis, mask)
        mask *= 2
    return value


def local(tokens, cotangent, lengths, w_in, w_out, w_gate_up, w_down, norm_gains, conv_kernel):
    nz, n_fs = lax.axis_size("tensor"), lax.axis_size("fsdp")
    me = lax.axis_index("fsdp")
    own_tokens, cot_rows = tokens[0], cotangent[0]

    in_first = fetch_shards(w_in, 1)
    out_first = fetch_shards(w_out, 0)
    gain_others = [swap(norm_gains, "fsdp", mask) for mask in range(1, n_fs)]
    before = shifted(own_tokens[-halo:], "context", 1)
    behind = shifted(own_tokens[:halo], "context", -1)
    in_second = swap_cores(in_first)
    out_second = swap_cores(out_first)
    gain_width = norm_gains.shape[1]
    gains = lax.dynamic_update_slice_in_dim(
        jnp.zeros((2, gain_width * n_fs), bf16), norm_gains, me * gain_width, 1
    )
    for mask in range(1, n_fs):
        gains = lax.dynamic_update_slice_in_dim(
            gains, gain_others[mask - 1], (me ^ mask) * gain_width, 1
        )
    gate_up_first = fetch_shards(after(w_gate_up, *in_first, *out_first), 1)
    down_first = fetch_shards(after(w_down, *gate_up_first), 0)
    gate_up_second = swap_cores(gate_up_first)
    down_second = swap_cores(down_first)
    whole_in = Assembled([w_in, *in_first, *in_second], 1, 1, n_fs)
    whole_out = Assembled([w_out, *out_first, *out_second], 1, 0, n_fs)
    whole_gate_up = Assembled([w_gate_up, *gate_up_first, *gate_up_second], 1, 1, n_fs)
    whole_down = Assembled([w_down, *down_first, *down_second], 1, 0, n_fs)

    result = mixer_forward(
        lengths, own_tokens, before, behind, gains[0:1], conv_kernel, whole_in, whole_out, nz
    )
    parts, (hidden_one, b_ext, c_ext, x_ext, gated) = result[:nz], result[nz:]
    others = tensor_swap(parts)
    first_sum, h2_own = first_norm(parts[0], others, own_tokens, gains[1:2])
    h2_others = tensor_swap([h2_own] * nz)

    result = feed_forward(h2_own, h2_others, cot_rows, whole_gate_up, whole_down, nz)
    parts, (hidden_two, grad_gate, grad_up, act) = result[:nz], result[nz:]
    grad_h2_others = tensor_swap(parts)

    gate_up = Reduction(
        jnp.stack([dot_left(hidden_two, grad_gate), dot_left(hidden_two, grad_up)]), 1, 1
    )
    down = Reduction(dot_left(act, cot_rows), 1, 0)
    gate_up.over_cores()
    down.over_cores()
    down_parts = down_product(act, whole_down, nz)

    grad_first, grad_first_b, grad_gain_two = norm_back(
        parts[0], grad_h2_others, first_sum, gains[1:2], cot_rows
    )
    grad_first_others = tensor_swap([grad_first_b] * nz)
    ahead = shifted(grad_first_b[:halo], "context", -1)
    aheads = [ahead, *tensor_swap([ahead] * nz)]

    down.over_fsdp()
    gate_up.over_fsdp()
    down_others = tensor_swap(down_parts)

    result = mixer_backward(
        lengths,
        grad_first_b,
        grad_first_others,
        aheads,
        b_ext,
        c_ext,
        x_ext,
        conv_kernel,
        whole_in,
        whole_out,
        nz,
    )
    parts, (grad_first_whole, grad_b, grad_c, grad_x, grad_taps) = result[:nz], result[nz:]
    grad_h1_others = tensor_swap(parts)
    out = Reduction(dot_left(gated, grad_first_whole), 1, 0)
    inp = Reduction(
        jnp.stack(
            [
                dot_left(hidden_one, grad_b),
                dot_left(hidden_one, grad_c),
                dot_left(hidden_one, grad_x),
            ]
        ),
        1,
        1,
    )
    out.over_cores()
    inp.over_cores()
    _, grad_tokens_b, grad_gain_one = norm_back(
        parts[0], grad_h1_others, own_tokens, gains[0:1], grad_first
    )
    grad_tokens_others = tensor_swap([grad_tokens_b] * nz)
    rows_out = add_rows(first_sum, down_parts[0], down_others)
    output_others = tensor_swap([rows_out] * nz)

    down.over_rest()
    down.spread_rest()
    gate_up.over_rest()
    gate_up.spread_rest()
    out.over_fsdp()
    inp.over_fsdp()
    out.over_rest()
    out.spread_rest()
    inp.over_rest()
    inp.spread_rest()
    down_total = down.spread_cores()
    gate_up_total = gate_up.spread_cores()
    out_total = out.spread_cores()
    in_total = inp.spread_cores()

    small = jnp.concatenate([grad_gain_one, grad_gain_two], axis=0)
    small = sum_blocks(small, tensor_swap([small] * nz))
    n_gain = small.size
    small = jnp.concatenate([small.reshape(-1), grad_taps.reshape(-1)])
    small = butterfly(butterfly(small, "context"), "fsdp")
    gains_total = lax.dynamic_slice_in_dim(
        small[:n_gain].reshape(2, -1), me * gain_width, gain_width, 1
    )
    kernel_total = small[n_gain:].reshape(grad_taps.shape)

    return (
        widen(rows_out, output_others, nz)[None],
        widen(grad_tokens_b, grad_tokens_others, nz)[None],
        in_total,
        out_total,
        gate_up_total,
        down_total,
        gains_total,
        kernel_total,
    )


def solution(mesh):
    placed = (
        P("fsdp", "context", None),
        P("fsdp", "context", None),
        P("fsdp", None),
        P(None, "fsdp", "tensor"),
        P("tensor", "fsdp"),
        P(None, "fsdp", "tensor"),
        P("tensor", "fsdp"),
        P(None, "fsdp"),
        P(None, "tensor"),
    )
    return jax.shard_map(
        lambda *args: local(*args),
        mesh=mesh,
        in_specs=placed,
        out_specs=(
            P("fsdp", "context", None),
            P("fsdp", "context", None),
            P(None, "fsdp", "tensor"),
            P("tensor", "fsdp"),
            P(None, "fsdp", "tensor"),
            P("tensor", "fsdp"),
            P(None, "fsdp"),
            P(None, "tensor"),
        ),
        check_vma=False,
    )
```

time: 959 us -> 409 us (0.43)
  waiting for transfers between devices: 811 us -> 211 us
  starting transfers between devices: 3.89 us -> 91.7 us
  Pallas kernels: 0 us -> 62.4 us
  matrix products: 54 us -> 11.6 us
  blocking collectives: 33.8 us -> 0 us
  between operations: 14.6 us -> 1.64 us
  other arithmetic: 23.9 us -> 12.7 us
    psum x4 -> x0, waiting for transfers between devices: 457 us -> none  [the longest x1 160 us: local(): lax.psum((pieces[0], pieces[1], pieces[2], pieces[3], pieces[4]), 'context')]
    reduce_scatter x4 -> x0, waiting for transfers between devices: 240 us -> none  [the longest x1 113 us: local(): lax.psum_scatter(term_gate_up, 'fsdp', scatter_dimension=1, tiled=True)]
    ppermute x2 -> x65, waiting for transfers between devices: 1.27 us -> 211 us  [the longest x62 211 us: swap(): lax.ppermute(block, axis, [(i, i ^ mask) for i in range(lax.axis_size(axi...]
    all_gather x3 -> x0, waiting for transfers between devices: 111 us -> none  [the longest x1 60 us: local(): lax.all_gather(w_gate_up, 'fsdp', axis=1, tiled=True)]
    ppermute x2 -> x65, starting transfers between devices: 3 us -> 91.7 us  [the longest x62 86.6 us: swap(): lax.ppermute(block, axis, [(i, i ^ mask) for i in range(lax.axis_size(axi...]
    pallas_call x0 -> x14, Pallas kernels: none -> 62.4 us  [call(): return kernel(*ins, *any_ins)]
    dot_general x21 -> x7, matrix products: 54 us -> 11.6 us  [dot_left(): lax.dot_general(a, b, (((0,), (0,)), ((), ())), preferred_element_type=f32)]
    psum x2 -> x0, blocking collectives: 19.5 us -> none  [the longest x1 13.1 us: local(): kernel_total = lax.psum(grad_kernel, ('fsdp', 'context'))]
  transfers between devices with their start and end apart: 14 -> 65, of which waited for: 12 -> 28; matrix products, arithmetic and copies ran while one was open for 5% -> 8% of each run, Pallas kernels for 0% -> 10%
where the time goes in v1:
time: 409 us; the launch traced here: 408 us
  waiting for transfers between devices  211 us (52%)
  starting transfers between devices  91.7 us (22%)
  Pallas kernels  62.4 us (15%)
  local copies, waits for them, and re-layouts  16.6 us (4%)
  other arithmetic  12.7 us (3%)
  matrix products  11.6 us (3%)
    ppermute x62, waiting for transfers between devices, swap(): lax.ppermute(block, axis, [(i, i ^ mask) for i in range(lax.axis_size(axi...  211 us
    ppermute x62, starting transfers between devices, swap(): lax.ppermute(block, axis, [(i, i ^ mask) for i in range(lax.axis_size(axi...  86.6 us
    pallas_call x14, Pallas kernels, call(): return kernel(*ins, *any_ins)  62.4 us
    dot_general x7, matrix products, dot_left(): lax.dot_general(a, b, (((0,), (0,)), ((), ())), preferred_element_type=f32)  11.6 us
  transfers between devices with their start and end apart: 65, of which 28 were waited for; matrix products, arithmetic and copies ran while one was open for 8% of the time, Pallas kernels for 10%

profile of v1, /device:TPU:0, one launch (start us, length us, event | category | flops | bytes accessed | tf_op | source)
XLA Modules:
  0.0 407.5 jit_solution(9039946113628484248)
XLA Ops:
  1.8 3.0 collective-permute-start.3
  5.8 10.9 %collective-permute-done.5.refs_10_.refs_17_ = bf16[128,512]{1,0:T(8,128)(2,1)S(1)} collective-permute-done((bf16[128,512]{1,0:T(8,128)(2,1)S(1)}, bf16[128,512]{1,0:T(8,128)(2,1)S(1)}, u32[]{:S(2)}, u32[]{:S(2)}) %collective-permute-start.5) | collective-permute-done | bytes 131104 | tf_op jit(solution)/shard_map/ppermute | solution.py:16
  20.4 25.2 %collective-permute-done.13.refs_6_ = bf16[2,256,1152]{2,1,0:T(8,128)(2,1)} collective-permute-done((bf16[2,256,1152]{2,1,0:T(8,128)(2,1)S(1)}, bf16[2,256,1152]{2,1,0:T(8,128)(2,1)}, u32[]{:S(2)}, u32[]{:S(2)}) %collective-permute-start.13) | collective-permute-done | bytes 1179680 | tf_op jit(solution)/shard_map/ppermute | solution.py:16
  54.8 4.6 %collective-permute-done.15.refs_9_.refs_2_ = bf16[576,512]{1,0:T(8,128)(2,1)S(1)} collective-permute-done((bf16[576,512]{1,0:T(8,128)(2,1)S(1)}, bf16[576,512]{1,0:T(8,128)(2,1)S(1)}, u32[]{:S(2)}, u32[]{:S(2)}) %collective-permute-start.15) | collective-permute-done | bytes 589856 | tf_op jit(solution)/shard_map/ppermute | solution.py:16
  60.2 6.2 %shard_map.152 = (bf16[128,1024]{1,0:T(8,128)(2,1)}, bf16[128,1024]{1,0:T(8,128)(2,1)}, bf16[128,1024]{1,0:T(8,128)(2,1)}, bf16[128,1024]{1,0:T(8,128)(2,1)}, bf...) custom-call(s32[1,4]{1,0:T(1,128)} %refs_0_.3, ...), custom_call_target="tpu_custom_call" | custom-call | flops 1073741824 | bytes 3214864 | tf_op jit(solution)/shard_map/pallas_call | solution.py:74
  67.8 2.6 collective-permute-start.8
  70.9 9.6 %collective-permute-done.7.refs_1_ = bf16[128,1024]{1,0:T(8,128)(2,1)S(1)} collective-permute-done((bf16[128,1024]{1,0:T(8,128)(2,1)}, bf16[128,1024]{1,0:T(8,128)(2,1)S(1)}, u32[]{:S(2)}, u32[]{:S(2)}) %collective-permute-start.7) | collective-permute-done | bytes 262176 | tf_op jit(solution)/shard_map/ppermute | solution.py:16
  80.6 8.8 %collective-permute-done.8.refs_2_ = bf16[128,1024]{1,0:T(8,128)(2,1)S(1)} collective-permute-done((bf16[128,1024]{1,0:T(8,128)(2,1)}, bf16[128,1024]{1,0:T(8,128)(2,1)S(1)}, u32[]{:S(2)}, u32[]{:S(2)}) %collective-permute-start.8) | collective-permute-done | bytes 262176 | tf_op jit(solution)/shard_map/ppermute | solution.py:16
  90.2 2.6 shard_map.153
  92.8 5.3 %collective-permute-start.10 = (bf16[128,1024]{1,0:T(8,128)(2,1)}, bf16[128,1024]{1,0:T(8,128)(2,1)S(1)}, u32[]{:S(2)}, u32[]{:S(2)}) collective-permute-start(bf16[128,1024]{1,0:T(8,128)(2,1)} %get-tuple-element.52.refs_0_), channel_id=1, source_target_pairs={{0,1},{1,0},{2,3},{3,2},{4,5},{5,4},{6,7},{7,6},{8,9},{9,8},{10,11... | collective-permute-start | bytes 786440 | tf_op jit(solution)/shard_map/ppermute | solution.py:16
  100.6 8.1 %collective-permute-done.10.refs_1_ = bf16[128,1024]{1,0:T(8,128)(2,1)S(1)} collective-permute-done((bf16[128,1024]{1,0:T(8,128)(2,1)}, bf16[128,1024]{1,0:T(8,128)(2,1)S(1)}, u32[]{:S(2)}, u32[]{:S(2)}) %collective-permute-start.10) | collective-permute-done | bytes 262176 | tf_op jit(solution)/shard_map/ppermute | solution.py:16
  108.7 10.9 %collective-permute-done.11.refs_2_ = bf16[128,1024]{1,0:T(8,128)(2,1)S(1)} collective-permute-done((bf16[128,1024]{1,0:T(8,128)(2,1)}, bf16[128,1024]{1,0:T(8,128)(2,1)S(1)}, u32[]{:S(2)}, u32[]{:S(2)}) %collective-permute-start.11) | collective-permute-done | bytes 262176 | tf_op jit(solution)/shard_map/ppermute | solution.py:16
  120.6 16.5 %shard_map.154 = (bf16[128,1024]{1,0:T(8,128)(2,1)}, bf16[128,1024]{1,0:T(8,128)(2,1)}, bf16[128,1024]{1,0:T(8,128)(2,1)}, bf16[128,1024]{1,0:T(8,128)(2,1)}, bf...) custom-call(bf16[128,1024]{1,0:T(8,128)(2,1)} %get-tuple-element.52., ...), custom_call_target="tpu_custom_call" | custom-call | flops 6039797760 | bytes 9175040 | tf_op jit(solution)/shard_map/pallas_call | solution.py:74
  137.1 4.3 %collective-permute-start.23 = (bf16[128,1024]{1,0:T(8,128)(2,1)}, bf16[128,1024]{1,0:T(8,128)(2,1)S(1)}, u32[]{:S(2)}, u32[]{:S(2)}) collective-permute-start(bf16[128,1024]{1,0:T(8,128)(2,1)} %get-tuple-element.61), channel_id=1, source_target_pairs={{0,1},{1,0},{2,3},{3,2},{4,5},{5,4},{6,7},{7,6},{8,9},{9,8},{10,11... | collective-permute-start | bytes 786440 | tf_op jit(solution)/shard_map/ppermute | solution.py:16
  143.9 3.3 fusion.17
  147.2 3.8 fusion.18
  151.0 11.8 %collective-permute-done.24.refs_2_ = bf16[128,1024]{1,0:T(8,128)(2,1)S(1)} collective-permute-done((bf16[128,1024]{1,0:T(8,128)(2,1)}, bf16[128,1024]{1,0:T(8,128)(2,1)S(1)}, u32[]{:S(2)}, u32[]{:S(2)}) %collective-permute-start.24) | collective-permute-done | bytes 262176 | tf_op jit(solution)/shard_map/ppermute | solution.py:16
  163.6 3.0 shard_map.158
  168.8 5.5 %shard_map.155 = (bf16[128,1024]{1,0:T(8,128)(2,1)}, bf16[128,1024]{1,0:T(8,128)(2,1)}, bf16[128,1024]{1,0:T(8,128)(2,1)}, bf16[128,1024]{1,0:T(8,128)(2,1)}) custom-call(bf16[512,1152]{1,0:T(8,128)(2,1)} %get-tuple-element.55.refs_0_, bf16[1152,512]{1,0:T(8,128)(2,1)} %refs_1_.1, bf16[576,512]{1,0:T(8,128)(2,1)} %copy-done.46, bf16[576,512]{1,0:T(8,128)(2,1)} %copy-done.47), custom_call_target="tpu_custom_call" | custom-call | flops 1207959552 | bytes 3538944 | tf_op jit(solution)/shard_map/pallas_call | solution.py:74
  174.3 3.4 collective-permute-start.17
  181.1 3.5 fusion.1
  184.6 5.3 %collective-permute-done.17.refs_2_ = bf16[128,1024]{1,0:T(8,128)(2,1)S(1)} collective-permute-done((bf16[128,1024]{1,0:T(8,128)(2,1)}, bf16[128,1024]{1,0:T(8,128)(2,1)S(1)}, u32[]{:S(2)}, u32[]{:S(2)}) %collective-permute-start.17) | collective-permute-done | bytes 262176 | tf_op jit(solution)/shard_map/ppermute | solution.py:16
  189.9 9.3 %collective-permute-done.18.refs_3_ = bf16[128,1024]{1,0:T(8,128)(2,1)S(1)} collective-permute-done((bf16[128,1024]{1,0:T(8,128)(2,1)}, bf16[128,1024]{1,0:T(8,128)(2,1)S(1)}, u32[]{:S(2)}, u32[]{:S(2)}) %collective-permute-start.18) | collective-permute-done | bytes 262176 | tf_op jit(solution)/shard_map/ppermute | solution.py:16
  199.3 2.5 collective-permute-start.28
  201.8 15.9 %collective-permute-start.31 = (bf16[16,1024]{1,0:T(8,128)(2,1)S(1)}, bf16[16,1024]{1,0:T(8,128)(2,1)S(1)}, u32[]{:S(2)}, u32[]{:S(2)}) collective-permute-start(bf16[16,1024]{1,0:T(8,128)(2,1)S(1)} %collective-permute-done.29.refs_5_), channel_id=1, source_target_pairs={{0,2},{1,3},{2,0},{3,1},{4,6},{5,7},{6,4},{7,5},{8,10},{9,11},{10,... | collective-permute-start | bytes 98312 | tf_op jit(solution)/shard_map/ppermute | solution.py:16
  219.2 9.4 %collective-permute-done.31.refs_7_ = bf16[16,1024]{1,0:T(8,128)(2,1)S(1)} collective-permute-done((bf16[16,1024]{1,0:T(8,128)(2,1)S(1)}, bf16[16,1024]{1,0:T(8,128)(2,1)S(1)}, u32[]{:S(2)}, u32[]{:S(2)}) %collective-permute-start.31) | collective-permute-done | bytes 32800 | tf_op jit(solution)/shard_map/ppermute | solution.py:16
  235.4 7.1 %shard_map.159 = (bf16[128,1024]{1,0:T(8,128)(2,1)}, bf16[128,1024]{1,0:T(8,128)(2,1)}, bf16[128,1024]{1,0:T(8,128)(2,1)}, bf16[128,1024]{1,0:T(8,128)(2,1)}, bf...) custom-call(s32[1,4]{1,0:T(1,128)} %refs_0_.3, ...), custom_call_target="tpu_custom_call" | custom-call | flops 1073741824 | bytes 4949520 | tf_op jit(solution)/shard_map/pallas_call | solution.py:74
  242.5 2.9 collective-permute-start.34
  252.1 3.9 collective-permute-done.33.refs_1_
  256.0 8.3 %collective-permute-done.34.refs_2_ = bf16[128,1024]{1,0:T(8,128)(2,1)} collective-permute-done((bf16[128,1024]{1,0:T(8,128)(2,1)}, bf16[128,1024]{1,0:T(8,128)(2,1)}, u32[]{:S(2)}, u32[]{:S(2)}) %collective-permute-start.34) | collective-permute-done | bytes 262176 | tf_op jit(solution)/shard_map/ppermute | solution.py:16
  264.2 3.0 shard_map.160
  267.9 5.0 %collective-permute-start.59 = (f32[2,1024]{1,0:T(2,128)S(1)}, f32[2,1024]{1,0:T(2,128)S(1)}, u32[]{:S(2)}, u32[]{:S(2)}) collective-permute-start(f32[2,1024]{1,0:T(2,128)S(1)} %pad_maximum_fusion.1), channel_id=1, source_target_pairs={{0,1},{1,0},{2,3},{3,2},{4,5},{5,4},{6,7},{7,6},{8,9},{9,8},{10,11... | collective-permute-start | bytes 24584 | tf_op jit(solution)/shard_map/ppermute | solution.py:16
  279.5 3.2 fusion.3
  286.3 3.0 collective-permute-done.63
  290.2 20.7 %collective-permute-done.45 = bf16[128,512]{1,0:T(8,128)(2,1)S(1)} collective-permute-done((bf16[128,512]{1,0:T(8,128)(2,1)S(1)}, bf16[128,512]{1,0:T(8,128)(2,1)S(1)}, u32[]{:S(2)}, u32[]{:S(2)}) %collective-permute-start.45) | collective-permute-done | bytes 131104 | tf_op jit(solution)/shard_map/ppermute | solution.py:16
  316.0 13.2 %collective-permute-done.55 = bf16[576,512]{1,0:T(8,128)(2,1)S(1)} collective-permute-done((bf16[576,512]{1,0:T(8,128)(2,1)S(1)}, bf16[576,512]{1,0:T(8,128)(2,1)S(1)}, u32[]{:S(2)}, u32[]{:S(2)}) %collective-permute-start.55) | collective-permute-done | bytes 589856 | tf_op jit(solution)/shard_map/ppermute | solution.py:16
  331.9 5.3 %collective-permute-done.40 = bf16[3,1,256,256]{3,2,0,1:T(8,128)(2,1)S(1)} collective-permute-done((bf16[3,1,256,256]{3,2,0,1:T(8,128)(2,1)S(1)}, bf16[3,1,256,256]{3,2,0,1:T(8,128)(2,1)S(1)}, u32[]{:S(2)}, u32[]{:S(2)}) %collective-permute-start.40) | collective-permute-done | bytes 393248 | tf_op jit(solution)/shard_map/ppermute | solution.py:16
  339.7 12.4 %collective-permute-done.52 = bf16[2,128,1152]{2,1,0:T(8,128)(2,1)S(1)} collective-permute-done((bf16[2,128,1152]{2,1,0:T(8,128)(2,1)S(1)}, bf16[2,128,1152]{2,1,0:T(8,128)(2,1)S(1)}, u32[]{:S(2)}, u32[]{:S(2)}) %collective-permute-start.52) | collective-permute-done | bytes 589856 | tf_op jit(solution)/shard_map/ppermute | solution.py:16
  352.3 4.0 collective-permute-done.41
  363.5 2.9 collective-permute-done.22.refs_3_
  368.4 4.3 %collective-permute-done.42 = bf16[3,128,256]{2,1,0:T(8,128)(2,1)S(1)} collective-permute-done((bf16[3,128,256]{2,1,0:T(8,128)(2,1)S(1)}, bf16[3,128,256]{2,1,0:T(8,128)(2,1)S(1)}, u32[]{:S(2)}, u32[]{:S(2)}) %collective-permute-start.42) | collective-permute-done | bytes 196640 | tf_op jit(solution)/shard_map/ppermute | solution.py:16
  372.7 4.2 %collective-permute-done.47 = bf16[64,512]{1,0:T(8,128)(2,1)S(1)} collective-permute-done((bf16[64,512]{1,0:T(8,128)(2,1)S(1)}, bf16[64,512]{1,0:T(8,128)(2,1)S(1)}, u32[]{:S(2)}, u32[]{:S(2)}) %collective-permute-start.47) | collective-permute-done | bytes 65568 | tf_op jit(solution)/shard_map/ppermute | solution.py:16
  377.0 3.0 collective-permute-start.38
  380.1 8.0 %collective-permute-done.37.refs_2_ = bf16[128,1024]{1,0:T(8,128)(2,1)S(1)} collective-permute-done((bf16[128,1024]{1,0:T(8,128)(2,1)}, bf16[128,1024]{1,0:T(8,128)(2,1)S(1)}, u32[]{:S(2)}, u32[]{:S(2)}) %collective-permute-start.37) | collective-permute-done | bytes 262176 | tf_op jit(solution)/shard_map/ppermute | solution.py:16
  388.8 2.6 shard_map.157
  392.7 2.6 shard_map.161
  399.5 2.8 shard_map.165
  403.4 4.1 %shard_map.164 = f32[2,512,1152]{2,1,0:T(8,128)} custom-call(bf16[2,256,1152]{2,1,0:T(8,128)(2,1)} %copy-done.3, bf16[2,256,1152]{2,1,0:T(8,128)(2,1)} %copy-done.10), custom_call_target="tpu_custom_call" | custom-call | bytes 2359296 | tf_op jit(solution)/shard_map/pallas_call | solution.py:74
  (275 shorter events, 83.8 us)
Async XLA Ops:
  1.8 15.0 %collective-permute-start.3 = (bf16[3,256,256]{2,1,0:T(8,128)(2,1)S(1)}, bf16[3,256,256]{2,1,0:T(8,128)(2,1)S(1)}, u32[]{:S(2)}, u32[]{:S(2)}) collective-permute-start(bf16[3,256,256]{2,1,0:T(8,128)(2,1)S(1)} %constant_dynamic-slice_fusion.4), channel_id=1, source_target_pairs={{0,16},{16,0},{1,17},{17,1},{2,18},{18,2},{3,19},{19,3},{4,20},{20... | collective-permute-start | bytes 1179656 | tf_op jit(solution)/shard_map/ppermute | solution.py:16
  5.7 11.0 %collective-permute-start.5 = (bf16[128,512]{1,0:T(8,128)(2,1)S(1)}, bf16[128,512]{1,0:T(8,128)(2,1)S(1)}, u32[]{:S(2)}, u32[]{:S(2)}) collective-permute-start(bf16[128,512]{1,0:T(8,128)(2,1)S(1)} %constant_dynamic-slice_fusion.3), channel_id=1, source_target_pairs={{0,16},{16,0},{1,17},{17,1},{2,18},{18,2},{3,19},{19,3},{4,20},{20... | collective-permute-start | bytes 393224 | tf_op jit(solution)/shard_map/ppermute | solution.py:16
  18.3 27.3 %collective-permute-start.13 = (bf16[2,256,1152]{2,1,0:T(8,128)(2,1)S(1)}, bf16[2,256,1152]{2,1,0:T(8,128)(2,1)}, u32[]{:S(2)}, u32[]{:S(2)}) collective-permute-start(bf16[2,256,1152]{2,1,0:T(8,128)(2,1)S(1)} %constant_dynamic-slice_fusion.2), channel_id=1, source_target_pairs={{0,16},{16,0},{1,17},{17,1},{2,18},{18,2},{3,19},{19,3},{4,20},{20... | collective-permute-start | bytes 3538952 | tf_op jit(solution)/shard_map/ppermute | solution.py:16
  20.1 31.5 %collective-permute-start.2 = (bf16[2,512]{1,0:T(2,128)(2,1)S(1)}, bf16[2,512]{1,0:T(2,128)(2,1)S(1)}, u32[]{:S(2)}, u32[]{:S(2)}) collective-permute-start(bf16[2,512]{1,0:T(2,128)(2,1)S(1)} %copy-done.45), channel_id=1, source_target_pairs={{0,16},{16,0},{1,17},{17,1},{2,18},{18,2},{3,19},{19,3},{4,20},{20... | collective-permute-start | bytes 6152 | tf_op jit(solution)/shard_map/ppermute | solution.py:16
  45.7 13.7 %collective-permute-start.15 = (bf16[576,512]{1,0:T(8,128)(2,1)S(1)}, bf16[576,512]{1,0:T(8,128)(2,1)S(1)}, u32[]{:S(2)}, u32[]{:S(2)}) collective-permute-start(bf16[576,512]{1,0:T(8,128)(2,1)S(1)} %constant_dynamic-slice_fusion.1), channel_id=1, source_target_pairs={{0,16},{16,0},{1,17},{17,1},{2,18},{18,2},{3,19},{19,3},{4,20},{20... | collective-permute-start | bytes 1769480 | tf_op jit(solution)/shard_map/ppermute | solution.py:16
  47.2 72.4 %collective-permute-start.14 = (bf16[2,256,1152]{2,1,0:T(8,128)(2,1)}, bf16[2,256,1152]{2,1,0:T(8,128)(2,1)}, u32[]{:S(2)}, u32[]{:S(2)}) collective-permute-start(bf16[2,256,1152]{2,1,0:T(8,128)(2,1)} %collective-permute-done.13.refs_6_), channel_id=1, source_target_pairs={{0,4},{4,0},{8,12},{12,8},{1,5},{5,1},{9,13},{13,9},{2,6},{6,2},{1... | collective-permute-start | bytes 3538952 | tf_op jit(solution)/shard_map/ppermute | solution.py:16
  59.4 60.2 %collective-permute-start.16 = (bf16[576,512]{1,0:T(8,128)(2,1)S(1)}, bf16[576,512]{1,0:T(8,128)(2,1)S(1)}, u32[]{:S(2)}, u32[]{:S(2)}) collective-permute-start(bf16[576,512]{1,0:T(8,128)(2,1)S(1)} %collective-permute-done.15.refs_9_.refs_2_), channel_id=1, source_target_pairs={{0,4},{4,0},{8,12},{12,8},{1,5},{5,1},{9,13},{13,9},{2,6},{6,2},{1... | collective-permute-start | bytes 1769480 | tf_op jit(solution)/shard_map/ppermute | solution.py:16
  66.5 14.1 %collective-permute-start.7 = (bf16[128,1024]{1,0:T(8,128)(2,1)}, bf16[128,1024]{1,0:T(8,128)(2,1)S(1)}, u32[]{:S(2)}, u32[]{:S(2)}) collective-permute-start(bf16[128,1024]{1,0:T(8,128)(2,1)} %get-tuple-element.48), channel_id=1, source_target_pairs={{0,1},{1,0},{2,3},{3,2},{4,5},{5,4},{6,7},{7,6},{8,9},{9,8},{10,11... | collective-permute-start | bytes 786440 | tf_op jit(solution)/shard_map/ppermute | solution.py:16
  67.8 21.6 %collective-permute-start.8 = (bf16[128,1024]{1,0:T(8,128)(2,1)}, bf16[128,1024]{1,0:T(8,128)(2,1)S(1)}, u32[]{:S(2)}, u32[]{:S(2)}) collective-permute-start(bf16[128,1024]{1,0:T(8,128)(2,1)} %get-tuple-element.49), channel_id=1, source_target_pairs={{0,2},{1,3},{2,0},{3,1},{4,6},{5,7},{6,4},{7,5},{8,10},{9,11},{10,... | collective-permute-start | bytes 786440 | tf_op jit(solution)/shard_map/ppermute | solution.py:16
  70.4 19.0 %collective-permute-start.9 = (bf16[128,1024]{1,0:T(8,128)(2,1)}, bf16[128,1024]{1,0:T(8,128)(2,1)S(1)}, u32[]{:S(2)}, u32[]{:S(2)}) collective-permute-start(bf16[128,1024]{1,0:T(8,128)(2,1)} %get-tuple-element.50), channel_id=1, source_target_pairs={{0,3},{1,2},{2,1},{3,0},{4,7},{5,6},{6,5},{7,4},{8,11},{9,10},{10,... | collective-permute-start | bytes 786440 | tf_op jit(solution)/shard_map/ppermute | solution.py:16
  92.8 15.9 %collective-permute-start.10 = (bf16[128,1024]{1,0:T(8,128)(2,1)}, bf16[128,1024]{1,0:T(8,128)(2,1)S(1)}, u32[]{:S(2)}, u32[]{:S(2)}) collective-permute-start(bf16[128,1024]{1,0:T(8,128)(2,1)} %get-tuple-element.52.refs_0_), channel_id=1, source_target_pairs={{0,1},{1,0},{2,3},{3,2},{4,5},{5,4},{6,7},{7,6},{8,9},{9,8},{10,11... | collective-permute-start | bytes 786440 | tf_op jit(solution)/shard_map/ppermute | solution.py:16
  98.1 21.5 %collective-permute-start.11 = (bf16[128,1024]{1,0:T(8,128)(2,1)}, bf16[128,1024]{1,0:T(8,128)(2,1)S(1)}, u32[]{:S(2)}, u32[]{:S(2)}) collective-permute-start(bf16[128,1024]{1,0:T(8,128)(2,1)} %get-tuple-element.52.refs_0_), channel_id=1, source_target_pairs={{0,2},{1,3},{2,0},{3,1},{4,6},{5,7},{6,4},{7,5},{8,10},{9,11},{10,... | collective-permute-start | bytes 786440 | tf_op jit(solution)/shard_map/ppermute | solution.py:16
  99.1 20.5 %collective-permute-start.12 = (bf16[128,1024]{1,0:T(8,128)(2,1)}, bf16[128,1024]{1,0:T(8,128)(2,1)S(1)}, u32[]{:S(2)}, u32[]{:S(2)}) collective-permute-start(bf16[128,1024]{1,0:T(8,128)(2,1)} %get-tuple-element.52.refs_0_), channel_id=1, source_target_pairs={{0,3},{1,2},{2,1},{3,0},{4,7},{5,6},{6,5},{7,4},{8,11},{9,10},{10,... | collective-permute-start | bytes 786440 | tf_op jit(solution)/shard_map/ppermute | solution.py:16
  137.1 13.8 %collective-permute-start.23 = (bf16[128,1024]{1,0:T(8,128)(2,1)}, bf16[128,1024]{1,0:T(8,128)(2,1)S(1)}, u32[]{:S(2)}, u32[]{:S(2)}) collective-permute-start(bf16[128,1024]{1,0:T(8,128)(2,1)} %get-tuple-element.61), channel_id=1, source_target_pairs={{0,1},{1,0},{2,3},{3,2},{4,5},{5,4},{6,7},{7,6},{8,9},{9,8},{10,11... | collective-permute-start | bytes 786440 | tf_op jit(solution)/shard_map/ppermute | solution.py:16
  141.4 21.4 %collective-permute-start.24 = (bf16[128,1024]{1,0:T(8,128)(2,1)}, bf16[128,1024]{1,0:T(8,128)(2,1)S(1)}, u32[]{:S(2)}, u32[]{:S(2)}) collective-permute-start(bf16[128,1024]{1,0:T(8,128)(2,1)} %get-tuple-element.62), channel_id=1, source_target_pairs={{0,2},{1,3},{2,0},{3,1},{4,6},{5,7},{6,4},{7,5},{8,10},{9,11},{10,... | collective-permute-start | bytes 786440 | tf_op jit(solution)/shard_map/ppermute | solution.py:16
  142.5 20.3 %collective-permute-start.25 = (bf16[128,1024]{1,0:T(8,128)(2,1)}, bf16[128,1024]{1,0:T(8,128)(2,1)S(1)}, u32[]{:S(2)}, u32[]{:S(2)}) collective-permute-start(bf16[128,1024]{1,0:T(8,128)(2,1)} %get-tuple-element.63), channel_id=1, source_target_pairs={{0,3},{1,2},{2,1},{3,0},{4,7},{5,6},{6,5},{7,4},{8,11},{9,10},{10,... | collective-permute-start | bytes 786440 | tf_op jit(solution)/shard_map/ppermute | solution.py:16
  167.3 12.8 %collective-permute-start.29 = (bf16[16,1024]{1,0:T(8,128)(2,1)S(1)}, bf16[16,1024]{1,0:T(8,128)(2,1)S(1)}, u32[]{:S(2)}, u32[]{:S(2)}) collective-permute-start(bf16[16,1024]{1,0:T(8,128)(2,1)S(1)} %slice.45), channel_id=1, source_target_pairs={{4,0},{8,4},{12,8},{5,1},{9,5},{13,9},{6,2},{10,6},{14,10},{7,3},{... | collective-permute-start | bytes 98312 | tf_op jit(solution)/shard_map/ppermute | solution.py:25
  174.3 15.7 %collective-permute-start.17 = (bf16[128,1024]{1,0:T(8,128)(2,1)}, bf16[128,1024]{1,0:T(8,128)(2,1)S(1)}, u32[]{:S(2)}, u32[]{:S(2)}) collective-permute-start(bf16[128,1024]{1,0:T(8,128)(2,1)} %get-tuple-element.57), channel_id=1, source_target_pairs={{0,1},{1,0},{2,3},{3,2},{4,5},{5,4},{6,7},{7,6},{8,9},{9,8},{10,11... | collective-permute-start | bytes 786440 | tf_op jit(solution)/shard_map/ppermute | solution.py:16
  177.6 21.6 %collective-permute-start.18 = (bf16[128,1024]{1,0:T(8,128)(2,1)}, bf16[128,1024]{1,0:T(8,128)(2,1)S(1)}, u32[]{:S(2)}, u32[]{:S(2)}) collective-permute-start(bf16[128,1024]{1,0:T(8,128)(2,1)} %get-tuple-element.58), channel_id=1, source_target_pairs={{0,2},{1,3},{2,0},{3,1},{4,6},{5,7},{6,4},{7,5},{8,10},{9,11},{10,... | collective-permute-start | bytes 786440 | tf_op jit(solution)/shard_map/ppermute | solution.py:16
  178.7 20.5 %collective-permute-start.19 = (bf16[128,1024]{1,0:T(8,128)(2,1)}, bf16[128,1024]{1,0:T(8,128)(2,1)S(1)}, u32[]{:S(2)}, u32[]{:S(2)}) collective-permute-start(bf16[128,1024]{1,0:T(8,128)(2,1)} %get-tuple-element.59), channel_id=1, source_target_pairs={{0,3},{1,2},{2,1},{3,0},{4,7},{5,6},{6,5},{7,4},{8,11},{9,10},{10,... | collective-permute-start | bytes 786440 | tf_op jit(solution)/shard_map/ppermute | solution.py:16
  180.1 21.7 %collective-permute-start.30 = (bf16[16,1024]{1,0:T(8,128)(2,1)S(1)}, bf16[16,1024]{1,0:T(8,128)(2,1)S(1)}, u32[]{:S(2)}, u32[]{:S(2)}) collective-permute-start(bf16[16,1024]{1,0:T(8,128)(2,1)S(1)} %collective-permute-done.29.refs_5_), channel_id=1, source_target_pairs={{0,1},{1,0},{2,3},{3,2},{4,5},{5,4},{6,7},{7,6},{8,9},{9,8},{10,11... | collective-permute-start | bytes 98312 | tf_op jit(solution)/shard_map/ppermute | solution.py:16
  184.6 94.8 %collective-permute-start.49 = (bf16[2,2,256,1152]{3,2,0,1:T(8,128)(2,1)}, bf16[2,2,256,1152]{3,2,0,1:T(8,128)(2,1)}, u32[]{:S(2)}, u32[]{:S(2)}) collective-permute-start(bf16[2,2,256,1152]{3,2,0,1:T(8,128)(2,1)} %fusion.1), channel_id=1, source_target_pairs={{0,4},{4,0},{8,12},{12,8},{1,5},{5,1},{9,13},{13,9},{2,6},{6,2},{1... | collective-permute-start | bytes 7077896 | tf_op jit(solution)/shard_map/ppermute | solution.py:16
  189.9 44.6 %collective-permute-start.26 = (bf16[128,1024]{1,0:T(8,128)(2,1)S(1)}, bf16[128,1024]{1,0:T(8,128)(2,1)S(1)}, u32[]{:S(2)}, u32[]{:S(2)}) collective-permute-start(bf16[128,1024]{1,0:T(8,128)(2,1)S(1)} %copy-done.15), channel_id=1, source_target_pairs={{0,1},{1,0},{2,3},{3,2},{4,5},{5,4},{6,7},{7,6},{8,9},{9,8},{10,11... | collective-permute-start | bytes 786440 | tf_op jit(solution)/shard_map/ppermute | solution.py:16
  199.2 35.3 %collective-permute-start.27 = (bf16[128,1024]{1,0:T(8,128)(2,1)S(1)}, bf16[128,1024]{1,0:T(8,128)(2,1)S(1)}, u32[]{:S(2)}, u32[]{:S(2)}) collective-permute-start(bf16[128,1024]{1,0:T(8,128)(2,1)S(1)} %copy-done.15), channel_id=1, source_target_pairs={{0,2},{1,3},{2,0},{3,1},{4,6},{5,7},{6,4},{7,5},{8,10},{9,11},{10,... | collective-permute-start | bytes 786440 | tf_op jit(solution)/shard_map/ppermute | solution.py:16
  199.3 35.3 %collective-permute-start.28 = (bf16[128,1024]{1,0:T(8,128)(2,1)S(1)}, bf16[128,1024]{1,0:T(8,128)(2,1)S(1)}, u32[]{:S(2)}, u32[]{:S(2)}) collective-permute-start(bf16[128,1024]{1,0:T(8,128)(2,1)S(1)} %copy-done.15), channel_id=1, source_target_pairs={{0,3},{1,2},{2,1},{3,0},{4,7},{5,6},{6,5},{7,4},{8,11},{9,10},{10,... | collective-permute-start | bytes 786440 | tf_op jit(solution)/shard_map/ppermute | solution.py:16
  201.8 26.8 %collective-permute-start.31 = (bf16[16,1024]{1,0:T(8,128)(2,1)S(1)}, bf16[16,1024]{1,0:T(8,128)(2,1)S(1)}, u32[]{:S(2)}, u32[]{:S(2)}) collective-permute-start(bf16[16,1024]{1,0:T(8,128)(2,1)S(1)} %collective-permute-done.29.refs_5_), channel_id=1, source_target_pairs={{0,2},{1,3},{2,0},{3,1},{4,6},{5,7},{6,4},{7,5},{8,10},{9,11},{10,... | collective-permute-start | bytes 98312 | tf_op jit(solution)/shard_map/ppermute | solution.py:16
  242.5 13.5 %collective-permute-start.33 = (bf16[128,1024]{1,0:T(8,128)(2,1)}, bf16[128,1024]{1,0:T(8,128)(2,1)}, u32[]{:S(2)}, u32[]{:S(2)}) collective-permute-start(bf16[128,1024]{1,0:T(8,128)(2,1)} %get-tuple-element.69), channel_id=1, source_target_pairs={{0,1},{1,0},{2,3},{3,2},{4,5},{5,4},{6,7},{7,6},{8,9},{9,8},{10,11... | collective-permute-start | bytes 786440 | tf_op jit(solution)/shard_map/ppermute | solution.py:16
  242.5 21.7 %collective-permute-start.34 = (bf16[128,1024]{1,0:T(8,128)(2,1)}, bf16[128,1024]{1,0:T(8,128)(2,1)}, u32[]{:S(2)}, u32[]{:S(2)}) collective-permute-start(bf16[128,1024]{1,0:T(8,128)(2,1)} %get-tuple-element.70), channel_id=1, source_target_pairs={{0,2},{1,3},{2,0},{3,1},{4,6},{5,7},{6,4},{7,5},{8,10},{9,11},{10,... | collective-permute-start | bytes 786440 | tf_op jit(solution)/shard_map/ppermute | solution.py:16
  245.4 18.8 %collective-permute-start.35 = (bf16[128,1024]{1,0:T(8,128)(2,1)}, bf16[128,1024]{1,0:T(8,128)(2,1)}, u32[]{:S(2)}, u32[]{:S(2)}) collective-permute-start(bf16[128,1024]{1,0:T(8,128)(2,1)} %get-tuple-element.71), channel_id=1, source_target_pairs={{0,3},{1,2},{2,1},{3,0},{4,7},{5,6},{6,5},{7,4},{8,11},{9,10},{10,... | collective-permute-start | bytes 786440 | tf_op jit(solution)/shard_map/ppermute | solution.py:16
  250.2 22.8 %collective-permute-start.44 = (bf16[128,1024]{1,0:T(8,128)(2,1)}, bf16[128,1024]{1,0:T(8,128)(2,1)S(1)}, u32[]{:S(2)}, u32[]{:S(2)}) collective-permute-start(bf16[128,1024]{1,0:T(8,128)(2,1)} %dynamic-slice_convert_fusion.7), channel_id=1, source_target_pairs={{0,4},{4,0},{8,12},{12,8},{1,5},{5,1},{9,13},{13,9},{2,6},{6,2},{1... | collective-permute-start | bytes 786440 | tf_op jit(solution)/shard_map/ppermute | solution.py:16
  256.0 55.0 %collective-permute-start.54 = (bf16[576,1024]{1,0:T(8,128)(2,1)}, bf16[576,1024]{1,0:T(8,128)(2,1)}, u32[]{:S(2)}, u32[]{:S(2)}) collective-permute-start(bf16[576,1024]{1,0:T(8,128)(2,1)} %dynamic-slice_convert_fusion), channel_id=1, source_target_pairs={{0,4},{4,0},{8,12},{12,8},{1,5},{5,1},{9,13},{13,9},{2,6},{6,2},{1... | collective-permute-start | bytes 3538952 | tf_op jit(solution)/shard_map/ppermute | solution.py:16
  276.5 84.7 %collective-permute-start.20 = (bf16[128,1024]{1,0:T(8,128)(2,1)}, bf16[128,1024]{1,0:T(8,128)(2,1)S(1)}, u32[]{:S(2)}, u32[]{:S(2)}) collective-permute-start(bf16[128,1024]{1,0:T(8,128)(2,1)} %shard_map.156.refs_0_), channel_id=1, source_target_pairs={{0,1},{1,0},{2,3},{3,2},{4,5},{5,4},{6,7},{7,6},{8,9},{9,8},{10,11... | collective-permute-start | bytes 786440 | tf_op jit(solution)/shard_map/ppermute | solution.py:16
  282.8 31.7 %collective-permute-start.50 = (bf16[2,1,256,1152]{3,2,0,1:T(8,128)(2,1)S(1)}, bf16[2,1,256,1152]{3,2,0,1:T(8,128)(2,1)S(1)}, u32[]{:S(2)}, u32[]{:S(2)}) collective-permute-start(bf16[2,1,256,1152]{3,2,0,1:T(8,128)(2,1)S(1)} %dynamic-slice_convert_fusion.1), channel_id=1, source_target_pairs={{0,16},{16,0},{1,17},{17,1},{2,18},{18,2},{3,19},{19,3},{4,20},{20... | collective-permute-start | bytes 3538952 | tf_op jit(solution)/shard_map/ppermute | solution.py:16
  284.4 26.5 %collective-permute-start.45 = (bf16[128,512]{1,0:T(8,128)(2,1)S(1)}, bf16[128,512]{1,0:T(8,128)(2,1)S(1)}, u32[]{:S(2)}, u32[]{:S(2)}) collective-permute-start(bf16[128,512]{1,0:T(8,128)(2,1)S(1)} %dynamic-slice_convert_fusion.9), channel_id=1, source_target_pairs={{0,16},{16,0},{1,17},{17,1},{2,18},{18,2},{3,19},{19,3},{4,20},{20... | collective-permute-start | bytes 393224 | tf_op jit(solution)/shard_map/ppermute | solution.py:16
  289.3 72.7 %collective-permute-start.21 = (bf16[128,1024]{1,0:T(8,128)(2,1)}, bf16[128,1024]{1,0:T(8,128)(2,1)S(1)}, u32[]{:S(2)}, u32[]{:S(2)}) collective-permute-start(bf16[128,1024]{1,0:T(8,128)(2,1)} %shard_map.156.refs_0_), channel_id=1, source_target_pairs={{0,2},{1,3},{2,0},{3,1},{4,6},{5,7},{6,4},{7,5},{8,10},{9,11},{10,... | collective-permute-start | bytes 786440 | tf_op jit(solution)/shard_map/ppermute | solution.py:16
  313.0 16.3 %collective-permute-start.55 = (bf16[576,512]{1,0:T(8,128)(2,1)S(1)}, bf16[576,512]{1,0:T(8,128)(2,1)S(1)}, u32[]{:S(2)}, u32[]{:S(2)}) collective-permute-start(bf16[576,512]{1,0:T(8,128)(2,1)S(1)} %dynamic-slice_convert_fusion.3), channel_id=1, source_target_pairs={{0,16},{16,0},{1,17},{17,1},{2,18},{18,2},{3,19},{19,3},{4,20},{20... | collective-permute-start | bytes 1769480 | tf_op jit(solution)/shard_map/ppermute | solution.py:16
  314.8 15.7 %collective-permute-start.51 = (bf16[2,128,1152]{2,1,0:T(8,128)(2,1)S(1)}, bf16[2,128,1152]{2,1,0:T(8,128)(2,1)S(1)}, u32[]{:S(2)}, u32[]{:S(2)}) collective-permute-start(bf16[2,128,1152]{2,1,0:T(8,128)(2,1)S(1)} %fusion.5), channel_id=1, source_target_pairs={{0,8},{4,12},{8,0},{12,4},{1,9},{5,13},{9,1},{13,5},{2,10},{6,14},... | collective-permute-start | bytes 1769480 | tf_op jit(solution)/shard_map/ppermute | solution.py:16
  315.4 21.8 %collective-permute-start.40 = (bf16[3,1,256,256]{3,2,0,1:T(8,128)(2,1)S(1)}, bf16[3,1,256,256]{3,2,0,1:T(8,128)(2,1)S(1)}, u32[]{:S(2)}, u32[]{:S(2)}) collective-permute-start(bf16[3,1,256,256]{3,2,0,1:T(8,128)(2,1)S(1)} %dynamic-slice_convert_fusion.5), channel_id=1, source_target_pairs={{0,16},{16,0},{1,17},{17,1},{2,18},{18,2},{3,19},{19,3},{4,20},{20... | collective-permute-start | bytes 1179656 | tf_op jit(solution)/shard_map/ppermute | solution.py:16
  330.8 21.2 %collective-permute-start.52 = (bf16[2,128,1152]{2,1,0:T(8,128)(2,1)S(1)}, bf16[2,128,1152]{2,1,0:T(8,128)(2,1)S(1)}, u32[]{:S(2)}, u32[]{:S(2)}) collective-permute-start(bf16[2,128,1152]{2,1,0:T(8,128)(2,1)S(1)} %get-tuple-element.89), channel_id=1, source_target_pairs={{0,8},{4,12},{8,0},{12,4},{1,9},{5,13},{9,1},{13,5},{2,10},{6,14},... | collective-permute-start | bytes 1769480 | tf_op jit(solution)/shard_map/ppermute | solution.py:16
  337.3 18.9 %collective-permute-start.41 = (bf16[3,128,256]{2,1,0:T(8,128)(2,1)S(1)}, bf16[3,128,256]{2,1,0:T(8,128)(2,1)S(1)}, u32[]{:S(2)}, u32[]{:S(2)}) collective-permute-start(bf16[3,128,256]{2,1,0:T(8,128)(2,1)S(1)} %fusion.7), channel_id=1, source_target_pairs={{0,8},{4,12},{8,0},{12,4},{1,9},{5,13},{9,1},{13,5},{2,10},{6,14},... | collective-permute-start | bytes 589832 | tf_op jit(solution)/shard_map/ppermute | solution.py:16
  339.6 21.2 %collective-permute-start.57 = (bf16[288,512]{1,0:T(8,128)(2,1)S(1)}, bf16[288,512]{1,0:T(8,128)(2,1)S(1)}, u32[]{:S(2)}, u32[]{:S(2)}) collective-permute-start(bf16[288,512]{1,0:T(8,128)(2,1)S(1)} %get-tuple-element.87), channel_id=1, source_target_pairs={{0,8},{4,12},{8,0},{12,4},{1,9},{5,13},{9,1},{13,5},{2,10},{6,14},... | collective-permute-start | bytes 884744 | tf_op jit(solution)/shard_map/ppermute | solution.py:16
  352.2 50.2 %collective-permute-start.53 = (bf16[2,256,1152]{2,1,0:T(8,128)(2,1)S(1)}, bf16[2,256,1152]{2,1,0:T(8,128)(2,1)S(1)}, u32[]{:S(2)}, u32[]{:S(2)}) collective-permute-start(bf16[2,256,1152]{2,1,0:T(8,128)(2,1)S(1)} %constant_dynamic-update-slice_fusion.2.own_ref), channel_id=1, source_target_pairs={{0,4},{4,0},{8,12},{12,8},{1,5},{5,1},{9,13},{13,9},{2,6},{6,2},{1... | collective-permute-start | bytes 3538952 | tf_op jit(solution)/shard_map/ppermute | solution.py:16
  356.3 10.1 %collective-permute-start.22 = (bf16[128,1024]{1,0:T(8,128)(2,1)}, bf16[128,1024]{1,0:T(8,128)(2,1)S(1)}, u32[]{:S(2)}, u32[]{:S(2)}) collective-permute-start(bf16[128,1024]{1,0:T(8,128)(2,1)} %shard_map.156.refs_0_), channel_id=1, source_target_pairs={{0,3},{1,2},{2,1},{3,0},{4,7},{5,6},{6,5},{7,4},{8,11},{9,10},{10,... | collective-permute-start | bytes 786440 | tf_op jit(solution)/shard_map/ppermute | solution.py:16
  361.2 15.8 %collective-permute-start.36 = (bf16[128,1024]{1,0:T(8,128)(2,1)}, bf16[128,1024]{1,0:T(8,128)(2,1)S(1)}, u32[]{:S(2)}, u32[]{:S(2)}) collective-permute-start(bf16[128,1024]{1,0:T(8,128)(2,1)} %get-tuple-element.73.refs_0_), channel_id=1, source_target_pairs={{0,1},{1,0},{2,3},{3,2},{4,5},{5,4},{6,7},{7,6},{8,9},{9,8},{10,11... | collective-permute-start | bytes 786440 | tf_op jit(solution)/shard_map/ppermute | solution.py:16
  366.3 33.2 %collective-permute-start.58 = (bf16[576,512]{1,0:T(8,128)(2,1)S(1)}, bf16[576,512]{1,0:T(8,128)(2,1)}, u32[]{:S(2)}, u32[]{:S(2)}) collective-permute-start(bf16[576,512]{1,0:T(8,128)(2,1)S(1)} %constant_dynamic-update-slice_fusion.own_ref), channel_id=1, source_target_pairs={{0,4},{4,0},{8,12},{12,8},{1,5},{5,1},{9,13},{13,9},{2,6},{6,2},{1... | collective-permute-start | bytes 1769480 | tf_op jit(solution)/shard_map/ppermute | solution.py:16
  366.5 21.6 %collective-permute-start.37 = (bf16[128,1024]{1,0:T(8,128)(2,1)}, bf16[128,1024]{1,0:T(8,128)(2,1)S(1)}, u32[]{:S(2)}, u32[]{:S(2)}) collective-permute-start(bf16[128,1024]{1,0:T(8,128)(2,1)} %get-tuple-element.73.refs_0_), channel_id=1, source_target_pairs={{0,2},{1,3},{2,0},{3,1},{4,6},{5,7},{6,4},{7,5},{8,10},{9,11},{10,... | collective-permute-start | bytes 786440 | tf_op jit(solution)/shard_map/ppermute | solution.py:16
  377.0 20.2 %collective-permute-start.43 = (bf16[3,256,256]{2,1,0:T(8,128)(2,1)S(1)}, bf16[3,256,256]{2,1,0:T(8,128)(2,1)}, u32[]{:S(2)}, u32[]{:S(2)}) collective-permute-start(bf16[3,256,256]{2,1,0:T(8,128)(2,1)S(1)} %constant_dynamic-update-slice_fusion.6.own_ref), channel_id=1, source_target_pairs={{0,4},{4,0},{8,12},{12,8},{1,5},{5,1},{9,13},{13,9},{2,6},{6,2},{1... | collective-permute-start | bytes 1179656 | tf_op jit(solution)/shard_map/ppermute | solution.py:16
  377.0 15.7 %collective-permute-start.38 = (bf16[128,1024]{1,0:T(8,128)(2,1)}, bf16[128,1024]{1,0:T(8,128)(2,1)}, u32[]{:S(2)}, u32[]{:S(2)}) collective-permute-start(bf16[128,1024]{1,0:T(8,128)(2,1)} %get-tuple-element.73.refs_0_), channel_id=1, source_target_pairs={{0,3},{1,2},{2,1},{3,0},{4,7},{5,6},{6,5},{7,4},{8,11},{9,10},{10,... | collective-permute-start | bytes 786440 | tf_op jit(solution)/shard_map/ppermute | solution.py:16
  (74 other events, 993.4 us)
